TPU v7x, 128 devices: a whole 4x4x4 slice. The times are simulated.
128 devices in a mesh: gx: 4 (over z_lo, core), gy: 4 (over x), gz: 8 (over y, z_hi).
Axes of the slice: x: 4, y: 4, z: 4 (z_hi: 2, z_lo: 2; z = z_hi * 2 + z_lo), core: 2. Of those that a mesh axis runs over, the one named last changes fastest.
Arguments:
- features: bfloat16 [32, 32, 128, 96], P('gx', 'gy', 'gz'), may hold values from -10 to 10
- ground: int32 [32, 32], P('gx', 'gy'), may hold values from 0 to 64, as said below
- thickness: int32 [32, 32], P('gx', 'gy'), may hold values from 1 to 64
- weight_one: bfloat16 [27, 96, 96], replicated, may hold values from -0.125 to 0.125
- weight_two: bfloat16 [27, 96, 96], replicated, may hold values from -0.125 to 0.125
- gains: float32 [2, 96], replicated, may hold values from 0.5 to 1.5
- shifts: float32 [2, 96], replicated, may hold values from -3 to 3
- cotangent: bfloat16 [32, 32, 128, 96], P('gx', 'gy', 'gz'), may hold values from -6 to 6
Outputs:
- result: bfloat16 [32, 32, 128, 96], P('gx', 'gy', 'gz')
- grad_features: bfloat16 [32, 32, 128, 96], P('gx', 'gy', 'gz')
- grad_one: float32 [27, 96, 96], replicated
- grad_two: float32 [27, 96, 96], replicated
- norm_grads: float32 [4, 96], replicated
Inputs may be any that keep to these rules, and one draw needn't show every extreme that they name: ground is constant over each aligned 8 x 8 footprint of vertical columns.
All inputs are finite; a program needn't handle non-finite values.
Results may differ from a plain program's by a relative error of at most 0.0058.
Values may be sent and summed in bfloat16 or wider, within the bound.
A program may use at most 128 MiB of HBM per device.

v0:
```python
import math

import jax
import jax.numpy as jnp
from jax import lax
from jax.sharding import PartitionSpec as P


def with_halo(block, sides, width):
    for axis, dim in sides:
        count = lax.axis_size(axis)
        forward = [(i, i + 1) for i in range(count - 1)]
        backward = [(target, source) for source, target in forward]
        low = lax.ppermute(
            lax.slice_in_dim(block, block.shape[dim] - width, None, axis=dim), axis, forward
        )
        high = lax.ppermute(lax.slice_in_dim(block, 0, width, axis=dim), axis, backward)
        block = jnp.concatenate([low, block, high], axis=dim)
    return block


def extend(block):
    return with_halo(block, (("gx", 0), ("gy", 1), ("gz", 2)), 1)


def window(padded, row_off, col_off, sizes, flipped):
    size_x, size_y, size_z = sizes
    channels = padded.shape[-1]
    pieces = []
    for depth in range(3):
        if flipped:
            start_x, start_y, start_z = (2 - row_off, 2 - col_off, 2 - depth)
        else:
            start_x, start_y, start_z = (row_off, col_off, depth)
        pieces.append(
            padded[
                :,
                start_x : start_x + size_x,
                start_y : start_y + size_y,
                start_z : start_z + size_z,
            ]
        )
    return jnp.concatenate(pieces, axis=-1).reshape(-1, 3 * channels)


def convolve(padded, stacked, sizes, flipped):
    total = None
    for row_off in range(3):
        for col_off in range(3):
            patch = window(padded, row_off, col_off, sizes, flipped)
            term = jnp.dot(patch, stacked[row_off, col_off], preferred_element_type=jnp.float32)
            total = term if total is None else total + term
    return total


def weight_terms(padded, grads, sizes):
    channels = padded.shape[-1]
    blocks = []
    for row_off in range(3):
        for col_off in range(3):
            patch = window(padded, row_off, col_off, sizes, False)
            product = lax.dot_general(
                patch, grads, (((0,), (0,)), ((), ())), preferred_element_type=jnp.float32
            )
            blocks.append(product.reshape(3, channels, channels))
    return jnp.stack(blocks).reshape(27, channels, channels)


def moments(values, mask_flat):
    totals, count = lax.psum((jnp.sum(values, axis=0), jnp.sum(mask_flat)), ("gx", "gy", "gz"))
    mean = totals / count
    deviation = (values - mean) * mask_flat[:, None]
    spread = lax.psum(jnp.sum(deviation * deviation, axis=0), ("gx", "gy", "gz"))
    var = spread / count
    return (mean, lax.rsqrt(var + 1e-05), count)


def norm_sums(grads, normed):
    return lax.psum((jnp.sum(grads, axis=0), jnp.sum(grads * normed, axis=0)), ("gx", "gy", "gz"))


def slope(pre):
    sig = jax.nn.sigmoid(pre)
    return sig * (1.0 + pre * (1.0 - sig))


def make_plan(inside, sizes):
    size_x, size_y, size_z = sizes
    brick_x, brick_y, brick_z = (size_x // 8, size_y // 8, size_z // 8)
    bricks = brick_x * brick_y * brick_z
    groups = lax.axis_size("gz")
    member = lax.axis_index("gz")
    occupied = (
        jnp.any(inside.reshape(brick_x, 8, brick_y, 8, brick_z, 8), axis=(1, 3, 5))
        .reshape(-1)
        .astype(jnp.int32)
    )
    counts = lax.all_gather(jnp.sum(occupied).reshape(1), "gz", axis=0, tiled=True)
    ends = jnp.cumsum(counts)
    starts = ends - counts
    order = jnp.arange(groups, dtype=jnp.int32)
    mine_start = jnp.sum(jnp.where(order == member, starts, 0))
    total = jnp.sum(counts)
    per_sender = -(-bricks // groups)
    height = size_z * groups
    span = (height // 2 + 6) // 8 + 1
    per_owner = -(-(brick_x * brick_y * span) // groups)
    local_rank = jnp.cumsum(occupied) - occupied
    owner = (mine_start + local_rank) % groups
    place = (local_rank - (owner - mine_start) % groups) // groups
    home = jnp.where(occupied > 0, owner * per_sender + place, 0)
    slots = jnp.arange(groups * per_sender, dtype=jnp.int32)
    hits = (home[None, :] == slots[:, None]) & (occupied[None, :] > 0)
    send_src = jnp.sum(jnp.where(hits, jnp.arange(bricks, dtype=jnp.int32)[None, :], 0), axis=1)
    send_ok = jnp.any(hits, axis=1)
    wanted = member + groups * jnp.arange(per_owner, dtype=jnp.int32)
    valid = wanted < total
    sender = jnp.minimum(
        jnp.sum((ends[None, :] <= wanted[:, None]).astype(jnp.int32), axis=1), groups - 1
    )
    sender_start = jnp.sum(jnp.where(order[None, :] == sender[:, None], starts[None, :], 0), axis=1)
    own_place = (wanted - sender_start - (member - sender_start) % groups) // groups
    own_src = jnp.where(valid, sender * per_sender + own_place, 0)
    back_hits = (own_src[None, :] == slots[:, None]) & valid[None, :]
    back_src = jnp.sum(
        jnp.where(back_hits, jnp.arange(per_owner, dtype=jnp.int32)[None, :], 0), axis=1
    )
    back_ok = jnp.any(back_hits, axis=1)
    return {
        "counts": (brick_x, brick_y, brick_z, groups, per_sender),
        "occupied": occupied,
        "home": home,
        "send_src": send_src,
        "send_ok": send_ok,
        "own_src": own_src,
        "valid": valid,
        "back_src": back_src,
        "back_ok": back_ok,
    }


def dispatch(padded, plan):
    brick_x, brick_y, brick_z, groups, per_sender = plan["counts"]
    channels = padded.shape[-1]
    pieces = []
    for index_z in range(brick_z):
        pieces.append(padded[0:10, 0:10, 8 * index_z : 8 * index_z + 10])
    stacked = jnp.stack(pieces)
    keep = plan["send_ok"].astype(jnp.bfloat16)[:, None, None, None, None]
    outgoing = (jnp.take(stacked, plan["send_src"], axis=0) * keep).reshape(
        groups, per_sender, 10, 10, 10, channels
    )
    arrived = lax.all_to_all(outgoing, "gz", split_axis=0, concat_axis=0, tiled=True).reshape(
        groups * per_sender, 10, 10, 10, channels
    )
    alive = plan["valid"].astype(jnp.bfloat16)[:, None, None, None, None]
    return jnp.take(arrived, plan["own_src"], axis=0) * alive


def collect(rows, plan):
    brick_x, brick_y, brick_z, groups, per_sender = plan["counts"]
    channels = rows.shape[-1]
    owned = rows.reshape(-1, 8, 8, 8, channels)
    keep = plan["back_ok"].astype(jnp.float32)[:, None, None, None, None]
    leaving = (jnp.take(owned, plan["back_src"], axis=0) * keep).reshape(
        groups, per_sender, 8, 8, 8, channels
    )
    returned = lax.all_to_all(leaving, "gz", split_axis=0, concat_axis=0, tiled=True).reshape(
        groups * per_sender, 8, 8, 8, channels
    )
    alive = plan["occupied"].astype(jnp.float32)[:, None, None, None, None]
    mine = jnp.take(returned, plan["home"], axis=0) * alive
    mine = mine.reshape(brick_x, brick_y, brick_z, 8, 8, 8, channels).transpose(0, 3, 1, 4, 2, 5, 6)
    return mine.reshape(-1, channels)


def layer(padded, stacked, flipped, plan):
    owned = dispatch(padded, plan)
    return (collect(convolve(owned, stacked, (8, 8, 8), flipped), plan), owned)


def weight_part(source, grads_kept):
    channels = source.shape[-1]
    centers = grads_kept[:, 1:9, 1:9, 1:9].reshape(-1, channels)
    return weight_terms(source, centers, (8, 8, 8))


def local(features, ground, thickness, weight_one, weight_two, gains, shifts, cotangent):
    size_x, size_y, size_z, channels = features.shape
    sizes = (size_x, size_y, size_z)
    level = lax.axis_index("gz") * size_z + jnp.arange(size_z, dtype=jnp.int32)
    inside = (level[None, None, :] >= ground[:, :, None]) & (
        level[None, None, :] < (ground + thickness)[:, :, None]
    )
    plan = make_plan(inside, sizes)
    mask_flat = inside.astype(jnp.float32).reshape(-1)
    mask_col = mask_flat[:, None]
    start = features * inside[..., None].astype(jnp.bfloat16)
    start_flat = start.reshape(-1, channels).astype(jnp.float32)
    forward_one = weight_one.reshape(3, 3, 3 * channels, channels)
    forward_two = weight_two.reshape(3, 3, 3 * channels, channels)
    backward_one = jnp.swapaxes(weight_one.reshape(3, 3, 3, channels, channels), 3, 4).reshape(
        3, 3, 3 * channels, channels
    )
    backward_two = jnp.swapaxes(weight_two.reshape(3, 3, 3, channels, channels), 3, 4).reshape(
        3, 3, 3 * channels, channels
    )
    conv_one, kept_start = layer(extend(start), forward_one, False, plan)
    conv_one = conv_one * mask_col
    mean_one, rstd_one, count = moments(conv_one, mask_flat)
    normal_one = (conv_one - mean_one) * rstd_one
    act_one = gains[0] * normal_one + shifts[0]
    hidden = (jax.nn.silu(act_one) * mask_col).astype(jnp.bfloat16)
    conv_two, kept_hidden = layer(
        extend(hidden.reshape(size_x, size_y, size_z, channels)), forward_two, False, plan
    )
    conv_two = conv_two * mask_col
    mean_two, rstd_two, count_again = moments(conv_two, mask_flat)
    normal_two = (conv_two - mean_two) * rstd_two
    act_two = gains[1] * normal_two + shifts[1] + start_flat
    result = (jax.nn.silu(act_two) * mask_col).astype(jnp.bfloat16).reshape(features.shape)
    d_two = cotangent.reshape(-1, channels).astype(jnp.float32) * mask_col * slope(act_two)
    sum_two, cross_two = norm_sums(d_two, normal_two)
    grad_y2 = (
        mask_col
        * gains[1]
        * rstd_two
        * (d_two - sum_two / count_again - normal_two * cross_two / count_again)
    ).astype(jnp.bfloat16)
    back_hidden, kept_grad2 = layer(
        extend(grad_y2.reshape(size_x, size_y, size_z, channels)), backward_two, True, plan
    )
    grad_w2 = weight_part(kept_hidden, kept_grad2)
    d_one = back_hidden * mask_col * slope(act_one)
    sum_one, cross_one = norm_sums(d_one, normal_one)
    grad_y1 = (
        mask_col * gains[0] * rstd_one * (d_one - sum_one / count - normal_one * cross_one / count)
    ).astype(jnp.bfloat16)
    back_start, kept_grad1 = layer(
        extend(grad_y1.reshape(size_x, size_y, size_z, channels)), backward_one, True, plan
    )
    grad_w1 = weight_part(kept_start, kept_grad1)
    grad_w1, grad_w2 = lax.psum((grad_w1, grad_w2), ("gx", "gy", "gz"))
    grad_features = (mask_col * (d_two + back_start)).astype(jnp.bfloat16).reshape(features.shape)
    total_cells = (
        size_x * lax.axis_size("gx") * size_y * lax.axis_size("gy") * size_z * lax.axis_size("gz")
    )
    scale = 1.0 / math.sqrt(total_cells / 8.0)
    norm_grads = jnp.stack([cross_one, sum_one, cross_two, sum_two]) * scale
    return (result, grad_features, grad_w1 * scale, grad_w2 * scale, norm_grads)


def solution(mesh):
    return jax.shard_map(
        local,
        mesh=mesh,
        in_specs=(
            P("gx", "gy", "gz", None),
            P("gx", "gy"),
            P("gx", "gy"),
            P(),
            P(),
            P(),
            P(),
            P("gx", "gy", "gz", None),
        ),
        out_specs=(P("gx", "gy", "gz", None), P("gx", "gy", "gz", None), P(), P(), P()),
        check_vma=False,
    )
```

profile of v0, /device:TPU:1, one launch (start us, length us, event | category | flops | bytes accessed | tf_op | source)
XLA Modules:
  0.0 1078.3 jit_solution(1146307342110098074)
XLA Ops:
  20.9 11.1 %all-reduce = s32[8]{0:T(128)S(1)} all-reduce(s32[8]{0:T(128)S(1)} %dynamic-update-slice), channel_id=1, replica_groups=mesh['gx'=4,'gy'=4,'gz'=8] {'gz'}, use_global_device_ids=true, to_apply=%add | all-reduce | flops 8 | bytes 64
  59.6 5.6 reshape.1330
  69.2 19.2 %all-to-all-done = bf16[8,2,48000]{2,1,0:T(2,128)(2,1)S(1)} async-done(((bf16[8,2,48000]{2,1,0:T(2,128)(2,1)}), bf16[8,2,48000]{2,1,0:T(2,128)(2,1)S(1)}, u32[]{:S(2)}, u32[]{:S(2)}) %all-to-all-start) | async-done | bytes 1536032 | tf_op jit(solution)/shard_map/all_to_all | solution.py:153
  88.3 6.0 reshape.1331
  124.0 28.5 %all-to-all-done.1 = f32[8,1,8,8,8,96]{5,4,3,2,1,0:T(8,128)S(1)} async-done(((f32[8,1,8,8,8,96]{5,4,3,2,1,0:T(8,128)}), f32[8,1,8,8,8,96]{5,4,3,2,1,0:T(8,128)S(1)}, u32[]{:S(2)}, u32[]{:S(2)}) %all-to-all-start.1) | async-done | bytes 1572896 | tf_op jit(solution)/shard_map/all_to_all | solution.py:168
  153.4 63.8 %all-reduce.3 = (f32[96]{0:T(128)S(1)}, f32[]{:T(128)}) all-reduce(f32[96]{0:T(128)S(1)} %get-tuple-element.26, f32[]{:T(128)} %fusion.69), channel_id=1, replica_groups=mesh['gx'=4,'gy'=4,'gz'=8] {'gx','gy','gz'}, use_global_device_ids=true, to_apply=%region_13.18 | all-reduce | flops 97 | bytes 776 | tf_op jit(solution)/shard_map/psum | solution.py:70
  218.0 63.2 %psum.82 = f32[96]{0:T(128)S(1)} all-reduce(f32[96]{0:T(128)S(1)} %multiply_reduce_fusion.3), channel_id=1, replica_groups=mesh['gx'=4,'gy'=4,'gz'=8] {'gx','gy','gz'}, use_global_device_ids=true, to_apply=%region_17.22 | all-reduce | flops 96 | bytes 768 | tf_op jit(solution)/shard_map/psum | solution.py:73
  313.7 6.9 reshape.1332
  320.6 24.6 %all_to_all.40 = bf16[8,2,48000]{2,1,0:T(2,128)(2,1)} all-to-all(bf16[8,2,48000]{2,1,0:T(2,128)(2,1)S(1)} %reshape.1332), channel_id=1, replica_groups=mesh['gx'=4,'gy'=4,'gz'=8] {'gz'}, dimensions={0} | all-to-all | bytes 3072000 | tf_op jit(solution)/shard_map/all_to_all | solution.py:153
  345.2 7.9 reshape.1333
  375.1 28.9 %all_to_all.41 = f32[8,1,8,8,8,96]{5,4,3,2,1,0:T(8,128)S(1)} all-to-all(f32[8,1,8,8,8,96]{5,4,3,2,1,0:T(8,128)S(1)} %fusion.6), channel_id=1, replica_groups=mesh['gx'=4,'gy'=4,'gz'=8] {'gz'}, dimensions={0} | all-to-all | bytes 3145728 | tf_op jit(solution)/shard_map/all_to_all | solution.py:168
  404.9 66.1 %psum.83 = f32[96]{0:T(128)S(1)} all-reduce(f32[96]{0:T(128)S(1)} %get-tuple-element.24), channel_id=1, replica_groups=mesh['gx'=4,'gy'=4,'gz'=8] {'gx','gy','gz'}, use_global_device_ids=true, to_apply=%region_19.24 | all-reduce | flops 96 | bytes 768 | tf_op jit(solution)/shard_map/psum | solution.py:70
  471.9 62.6 %psum.84 = f32[96]{0:T(128)S(1)} all-reduce(f32[96]{0:T(128)S(1)} %multiply_reduce_fusion.2), channel_id=1, replica_groups=mesh['gx'=4,'gy'=4,'gz'=8] {'gx','gy','gz'}, use_global_device_ids=true, to_apply=%region_21.26 | all-reduce | flops 96 | bytes 768 | tf_op jit(solution)/shard_map/psum | solution.py:73
  536.4 64.1 %all-reduce.2 = (f32[96]{0:T(128)S(1)}, f32[96]{0:T(128)S(1)}) all-reduce(f32[96]{0:T(128)S(1)} %get-tuple-element.12, f32[96]{0:T(128)S(1)} %get-tuple-element.11), channel_id=1, replica_groups=mesh['gx'=4,'gy'=4,'gz'=8] {'gx','gy','gz'}, use_global_device_ids=true, to_apply=%region_25.30 | all-reduce | flops 192 | bytes 1536 | tf_op jit(solution)/shard_map/psum | solution.py:79
  633.4 7.9 reshape.1334
  647.1 19.8 %all-to-all-done.4 = bf16[8,2,48000]{2,1,0:T(2,128)(2,1)S(1)} async-done(((bf16[8,2,48000]{2,1,0:T(2,128)(2,1)}), bf16[8,2,48000]{2,1,0:T(2,128)(2,1)S(1)}, u32[]{:S(2)}, u32[]{:S(2)}) %all-to-all-start.4) | async-done | bytes 1536032 | tf_op jit(solution)/shard_map/all_to_all | solution.py:153
  666.9 6.0 reshape.1335
  721.2 6.0 all-to-all-done.5
  730.1 64.9 %all-reduce.1 = (f32[96]{0:T(128)S(1)}, f32[96]{0:T(128)S(1)}) all-reduce(f32[96]{0:T(128)S(1)} %get-tuple-element.10, f32[96]{0:T(128)S(1)} %get-tuple-element.9), channel_id=1, replica_groups=mesh['gx'=4,'gy'=4,'gz'=8] {'gx','gy','gz'}, use_global_device_ids=true, to_apply=%region_29.34 | all-reduce | flops 192 | bytes 1536 | tf_op jit(solution)/shard_map/psum | solution.py:79
  828.6 7.9 reshape.1336
  836.5 5.6 all-to-all-start.6
  850.6 12.3 %all-to-all-done.6 = bf16[8,2,48000]{2,1,0:T(2,128)(2,1)S(1)} async-done(((bf16[8,2,48000]{2,1,0:T(2,128)(2,1)}), bf16[8,2,48000]{2,1,0:T(2,128)(2,1)S(1)}, u32[]{:S(2)}, u32[]{:S(2)}) %all-to-all-start.6) | async-done | bytes 1536032 | tf_op jit(solution)/shard_map/all_to_all | solution.py:153
  862.9 6.0 reshape.1337
  901.6 164.0 %all-reduce.7.cloned.1.call-done = (f32[27,96,96]{2,1,0:T(8,128)}, f32[27,96,96]{2,1,0:T(8,128)}) async-done(((f32[27,96,96]{2,1,0:T(8,128)}, f32[27,96,96]{2,1,0:T(8,128)}), (f32[27,96,96]{2,1,0:T(8,128)}, f32[27,96,96]{2,1,0:T(8,128)})) %all-reduce.7.cloned.1.call-update) | async-done | bytes 1990672 | tf_op jit(solution)/shard_map/psum | solution.py:243
  (468 shorter events, 303.0 us)
Async XLA Ops:
  9.9 25.1 %collective-permute-start = (bf16[1,8,16,96]{3,2,1,0:T(8,128)(2,1)S(1)}, bf16[1,8,16,96]{3,2,1,0:T(8,128)(2,1)S(1)}, u32[]{:S(2)}, u32[]{:S(2)}) collective-permute-start(bf16[1,8,16,96]{3,2,1,0:T(8,128)(2,1)S(1)} %get-tuple-element.175), channel_id=1, source_target_pairs={{0,32},{32,64},{64,96},{1,33},{33,65},{65,97},{2,34},{34,66},{66,9... | collective-permute-start | bytes 73736 | tf_op jit(solution)/shard_map/ppermute | solution.py:14
  14.8 20.2 %collective-permute-start.1 = (bf16[1,8,16,96]{3,2,1,0:T(8,128)(2,1)S(1)}, bf16[1,8,16,96]{3,2,1,0:T(8,128)(2,1)S(1)}, u32[]{:S(2)}, u32[]{:S(2)}) collective-permute-start(bf16[1,8,16,96]{3,2,1,0:T(8,128)(2,1)S(1)} %get-tuple-element.176), channel_id=1, source_target_pairs={{32,0},{64,32},{96,64},{33,1},{65,33},{97,65},{34,2},{66,34},{98,6... | collective-permute-start | bytes 73736 | tf_op jit(solution)/shard_map/ppermute | solution.py:17
  38.1 4.7 collective-permute-start.3
  43.0 6.0 collective-permute-start.4
  47.7 6.4 collective-permute-start.5
  65.2 23.1 %all-to-all-start = ((bf16[8,2,48000]{2,1,0:T(2,128)(2,1)}), bf16[8,2,48000]{2,1,0:T(2,128)(2,1)S(1)}, u32[]{:S(2)}, u32[]{:S(2)}) async-start(bf16[8,2,48000]{2,1,0:T(2,128)(2,1)} %reshape.1330), calls=%async_computation | async-start | bytes 3072000 | tf_op jit(solution)/shard_map/all_to_all | solution.py:153
  117.6 34.8 %all-to-all-start.1 = ((f32[8,1,8,8,8,96]{5,4,3,2,1,0:T(8,128)}), f32[8,1,8,8,8,96]{5,4,3,2,1,0:T(8,128)S(1)}, u32[]{:S(2)}, u32[]{:S(2)}) async-start(f32[8,1,8,8,8,96]{5,4,3,2,1,0:T(8,128)} %fusion.7), calls=%async_computation.1 | async-start | bytes 4194304 | tf_op jit(solution)/shard_map/all_to_all | solution.py:168
  282.2 6.1 collective-permute-start.7
  291.5 5.2 collective-permute-start.9
  296.8 4.6 collective-permute-start.10
  300.1 6.4 collective-permute-start.11
  602.4 6.5 collective-permute-start.13
  610.4 5.6 collective-permute-start.15
  616.1 4.7 collective-permute-start.16
  619.4 6.7 collective-permute-start.17
  641.3 25.6 %all-to-all-start.4 = ((bf16[8,2,48000]{2,1,0:T(2,128)(2,1)}), bf16[8,2,48000]{2,1,0:T(2,128)(2,1)S(1)}, u32[]{:S(2)}, u32[]{:S(2)}) async-start(bf16[8,2,48000]{2,1,0:T(2,128)(2,1)} %reshape.1334), calls=%async_computation.4 | async-start | bytes 3072000 | tf_op jit(solution)/shard_map/all_to_all | solution.py:153
  693.2 34.0 %all-to-all-start.5 = ((f32[8,1,8,8,8,96]{5,4,3,2,1,0:T(8,128)}), f32[8,1,8,8,8,96]{5,4,3,2,1,0:T(8,128)}, u32[]{:S(2)}, u32[]{:S(2)}) async-start(f32[8,1,8,8,8,96]{5,4,3,2,1,0:T(8,128)} %fusion.5), calls=%async_computation.5 | async-start | bytes 4194304 | tf_op jit(solution)/shard_map/all_to_all | solution.py:168
  797.0 6.9 collective-permute-start.19
  806.2 5.3 collective-permute-start.21
  811.6 5.5 collective-permute-start.22
  814.9 6.4 collective-permute-start.23
  836.5 26.4 %all-to-all-start.6 = ((bf16[8,2,48000]{2,1,0:T(2,128)(2,1)}), bf16[8,2,48000]{2,1,0:T(2,128)(2,1)S(1)}, u32[]{:S(2)}, u32[]{:S(2)}) async-start(bf16[8,2,48000]{2,1,0:T(2,128)(2,1)} %reshape.1336), calls=%async_computation.6 | async-start | bytes 3072000 | tf_op jit(solution)/shard_map/all_to_all | solution.py:153
  842.1 223.5 %all-reduce.7.cloned.1.call-start = ((), (), s32[]{:S(2)}) async-start(), calls=%async_computation.8 | async-start | bytes 5308416 | tf_op jit(solution)/shard_map/psum | solution.py:243
  897.1 172.3 %all-to-all-start.7 = ((f32[8,1,8,8,8,96]{5,4,3,2,1,0:T(8,128)}), f32[8,1,8,8,8,96]{5,4,3,2,1,0:T(8,128)S(1)}, u32[]{:S(2)}, u32[]{:S(2)}) async-start(f32[8,1,8,8,8,96]{5,4,3,2,1,0:T(8,128)} %fusion.4), calls=%async_computation.7 | async-start | bytes 4194304 | tf_op jit(solution)/shard_map/all_to_all | solution.py:168
  (95 other events, 5048.6 us)
Sparse Core Ops, SparseCore 0:
  894.9 170.6 all-reduce.6
where the time goes:
time: 1090 us; the launch traced here: 1080 us
  blocking collectives  449 us (41%)
  waiting for transfers between devices  284 us (26%)
  local copies, waits for them, and re-layouts  118 us (11%)
  starting transfers between devices  87.7 us (8%)
  other arithmetic  62.7 us (6%)
  matrix products  60 us (6%)
  between operations  16.5 us (2%)
    psum x1, waiting for transfers between devices, local(): grad_w1, grad_w2 = lax.psum((grad_w1, grad_w2), ('gx', 'gy', 'gz'))  164 us
    psum x2, blocking collectives, moments(): lax.psum((jnp.sum(values, axis=0), jnp.sum(mask_flat)), ('gx', 'gy', 'gz'))  130 us
    psum x2, blocking collectives, norm_sums(): lax.psum((jnp.sum(grads, axis=0), jnp.sum(grads * normed, axis=0)), ('gx'...  129 us
    psum x2, blocking collectives, moments(): lax.psum(jnp.sum(deviation * deviation, axis=0), ('gx', 'gy', 'gz'))  126 us
    unnamed x189, local copies, waits for them, and re-layouts  62.3 us
    all_to_all x3, waiting for transfers between devices, dispatch(): lax.all_to_all(outgoing, 'gz', split_axis=0, concat_axis=0, tiled=True)  51.3 us
    dot_general x36, matrix products, convolve(): jnp.dot(patch, stacked[row_off, col_off], preferred_element_type=jnp.floa...  44.9 us
    ppermute x12, starting transfers between devices, with_halo(): lax.ppermute(lax.slice_in_dim(block, block.shape[dim] - width, None, axis...  37.7 us
  transfers between devices with their start and end apart: 31, of which 18 were waited for; matrix products, arithmetic and copies ran while one was open for 5% of the time, Pallas kernels for 0%

commit v1 on v0

v1 whole, which is shorter than its diff:
```python
import functools
import math

import jax
import jax.numpy as jnp
from jax import lax
from jax.experimental import pallas as pl
from jax.experimental.pallas import tpu as pltpu
from jax.sharding import PartitionSpec as P

MESH = pl.DeviceIdType.MESH
F32 = jnp.float32
BF16 = jnp.bfloat16
L = 128
SIDES = [(dx, dy) for dx in (-1, 0, 1) for dy in (-1, 0, 1) if (dx, dy) != (0, 0)]


def sigmoid(v):
    return 1.0 / (1.0 + jnp.exp(-v))


def body(
    dims,
    feat_ref, ground_ref, thick_ref, w1_ref, w2_ref, gains_ref, shifts_ref, cot_ref,
    result_ref, gfeat_ref, g1_ref, g2_ref, norm_ref,
    S, CT, Y1, Y2, D1, MK, N1, N2, D2,
    ZS, ZR, MZ, NZ1, NZ2, DZ2,
    V, PS, PH, PD2, PD1, DT, W1, W2, T1, T2, GS,
    STS, RX, RY, RZ,
    GA, GC, GB, GY, GD, GZ, GE, GX, GF,
    hs, hr, zs, zr, ss, sr, gs, gr,
):
    NGX, NGY, NGZ, X, Y, Z, C, seg = dims
    XE, YE = X + 2, Y + 2
    gx, gy, gz = lax.axis_index("gx"), lax.axis_index("gy"), lax.axis_index("gz")
    nz_lo, n_y = NGX // 2, NGZ // 2
    core, z_lo = gx % 2, gx // 2
    row_y, z_hi = gz // 2, gz % 2
    n_z = nz_lo * 2
    pos_z = z_hi * nz_lo + z_lo

    def dev(ax, ay, az):
        return (ax, ay, az)

    def peer_x(j):
        return dev((gx + j) % NGX, gy, gz)

    def peer_y(j):
        return dev(gx, (gy + j) % NGY, gz)

    def peer_z(j):
        return dev(gx, gy, (gz + j) % NGZ)

    def side(dx, dy):
        return dev((gx + dx + NGX) % NGX, (gy + dy + NGY) % NGY, gz)

    def grad_y(j):
        return dev(gx, gy, ((row_y + j) % n_y) * 2 + z_hi)

    def grad_z(j):
        other = (pos_z + j) % n_z
        return dev((other % nz_lo) * 2 + core, gy, row_y * 2 + other // nz_lo)

    partner = dev(z_lo * 2 + 1 - core, gy, gz)

    greet = [peer_x(j) for j in range(1, NGX)]
    greet += [peer_y(j) for j in range(1, NGY)]
    greet += [peer_z(j) for j in range(1, NGZ)]
    greet += [side(dx, dy) for dx, dy in SIDES if dx and dy]
    greet += [grad_z(j) for j in range(1, n_z)]
    barrier = pltpu.get_barrier_semaphore()
    for other in greet:
        pl.semaphore_signal(barrier, inc=1, device_id=other, device_id_type=MESH)

    for ref in (W1, W2, T1, T2, GS):
        ref[...] = jnp.zeros(ref.shape, ref.dtype)
    GS[0:2, 0:C] = gains_ref[...]
    GS[2:4, 0:C] = shifts_ref[...]

    def load_block(x, carry):
        level = lax.broadcasted_iota(jnp.int32, (Z, L), 0) + gz * Z
        for y in range(Y):
            low = ground_ref[x, y]
            high = low + thick_ref[x, y]
            m = jnp.where((level >= low) & (level < high), 1.0, 0.0).astype(F32)
            S[1 + x, 1 + y] = m
            S[1 + x, 1 + y, :, 0:C] = m[:, 0:C] * feat_ref[x, y].astype(F32)
            CT[1 + x, 1 + y] = jnp.zeros((Z, L), F32)
            CT[1 + x, 1 + y, :, 0:C] = cot_ref[x, y].astype(F32)
        return carry

    lax.fori_loop(0, X, load_block, 0)
    pl.semaphore_wait(barrier, len(greet))

    def cut(d, n, sending):
        if d == 0:
            return pl.ds(1, n)
        if sending:
            return pl.ds(n if d > 0 else 1, 1)
        return pl.ds(0 if d > 0 else n + 1, 1)

    def plane_copies(q, ref):
        out = []
        for k, (dx, dy) in enumerate(SIDES):
            out.append(
                pltpu.make_async_remote_copy(
                    src_ref=ref.at[cut(dx, X, True), cut(dy, Y, True)],
                    dst_ref=ref.at[cut(dx, X, False), cut(dy, Y, False)],
                    send_sem=hs.at[q, k],
                    recv_sem=hr.at[q, k],
                    device_id=side(dx, dy),
                    device_id_type=MESH,
                )
            )
        return out

    def face_copies(q):
        down = dev(gx, gy, (gz + NGZ - 1) % NGZ)
        up = dev(gx, gy, (gz + 1) % NGZ)
        out = []
        for k, other in ((0, down), (1, up)):
            out.append(
                pltpu.make_async_remote_copy(
                    src_ref=ZS.at[q, k],
                    dst_ref=ZR.at[q, 1 - k],
                    send_sem=zs.at[q, k],
                    recv_sem=zr.at[q, k],
                    device_id=other,
                    device_id_type=MESH,
                )
            )
        return out

    def start_all(copies):
        for c in copies:
            c.start()

    def wait_all(copies):
        for c in copies:
            c.wait()

    def send_faces(q, ref):
        def one(x, carry):
            ZS[q, 0, x] = ref[x, :, 0, :]
            ZS[q, 1, x] = ref[x, :, Z - 1, :]
            return carry

        lax.fori_loop(0, XE, one, 0)
        start_all(face_copies(q))

    def sum_copies(k, axis):
        n, me, peer, land = (
            (NGX, gx, peer_x, RX), (NGY, gy, peer_y, RY), (NGZ, gz, peer_z, RZ)
        )[axis]
        base = (0, NGX, NGX + NGY)[axis]
        out = []
        for j in range(1, n):
            out.append(
                pltpu.make_async_remote_copy(
                    src_ref=STS.at[k, axis],
                    dst_ref=land.at[k, me],
                    send_sem=ss.at[k, base + j],
                    recv_sem=sr.at[k, base + j],
                    device_id=peer(j),
                    device_id_type=MESH,
                )
            )
        return out

    def sum_start(k, axis, rows):
        at = lax.broadcasted_iota(jnp.int32, (8, L), 0)
        tile = jnp.zeros((8, L), F32)
        for i, row in enumerate(rows):
            tile = jnp.where(at == i, jnp.broadcast_to(row, (8, L)), tile)
        STS[k, axis] = tile
        me, land = ((gx, RX), (gy, RY), (gz, RZ))[axis]
        land[k, me] = tile
        start_all(sum_copies(k, axis))

    def sum_wait(k, axis, spread):
        n, land = ((NGX, RX), (NGY, RY), (NGZ, RZ))[axis]
        wait_all(sum_copies(k, axis))
        tiles = [land[k, i] for i in range(n)]
        rows = [[t[i : i + 1] for t in tiles] for i in range(3)]
        first = functools.reduce(jnp.add, rows[0])
        second = functools.reduce(jnp.add, rows[1])
        if not spread:
            return [first, second]
        count = functools.reduce(jnp.add, rows[2])
        mean = first / jnp.maximum(count, 1.0)
        for s, m in zip(rows[0], rows[2]):
            off = s / jnp.maximum(m, 1.0) - mean
            second = second + m * off * off
        return [first, second, count]

    def put(dest, x, main, low, high):
        V[:, 8 : 8 + Z, :] = main
        for y in range(YE):
            V[y, 7:8, :] = low[y : y + 1]
            V[y, 8 + Z : 9 + Z, :] = high[y : y + 1]
        for c in range(3):
            dest[x, :, :, c * L : (c + 1) * L] = V[:, 7 + c : 7 + c + Z, :].astype(BF16)

    H = X // 2

    def convolve(src, weights, flipped, finish):
        def half(h, carry):
            total = None
            for k0 in range(0, 9, 2):
                parts = []
                for k in range(k0, min(k0 + 2, 9)):
                    a, b = k // 3, k % 3
                    if flipped:
                        a, b = 2 - a, 2 - b
                    parts.append(
                        src[pl.ds(h * H + a, H), b : b + Y, :, :].reshape(H * Y * Z, 3 * L)
                    )
                left = jnp.concatenate(parts, axis=1) if len(parts) > 1 else parts[0]
                right = weights[k0 * 3 * L : (k0 * 3 + 3 * len(parts)) * L, :]
                term = jnp.dot(left, right, preferred_element_type=F32)
                total = term if total is None else total + term
            finish(h, total.reshape(H, Y, Z, L))
            return carry

        lax.fori_loop(0, 2, half, 0)

    def own(ref, h):
        return ref[pl.ds(1 + h * H, H), 1 : 1 + Y, :, :]

    def local_sum(terms):
        def one(x, carry):
            return tuple(c + jnp.sum(t, axis=0) for c, t in zip(carry, terms(1 + x)))

        zero = tuple(jnp.zeros((Z, L), F32) for _ in terms(1))
        out = lax.fori_loop(0, X, one, zero)
        return [jnp.sum(v, axis=0, keepdims=True) for v in out]

    def mid(ref, x):
        return ref[x, 1 : 1 + Y, :, :]

    def products(g, src, dy):
        flat = dy[1 : 1 + X, 1 : 1 + Y, :, L : 2 * L].reshape(X * Y * Z, L)
        DT[...] = flat.T

        def one(k, carry):
            a, b = k // 3, k % 3
            patch = src[pl.ds(a, X), pl.ds(b, Y), :, :].reshape(X * Y * Z, 3 * L)
            out = jnp.dot(DT[...], patch, preferred_element_type=F32)
            for c in range(3):
                GA[g, pl.ds(pl.multiple_of((3 * k + c) * C, 8), C), :] = (
                    out[:, c * L : (c + 1) * L].T[0:C]
                )
            return carry

        lax.fori_loop(0, 9, one, 0)

    len_z = seg
    len_y = seg * n_z
    len_c = seg * n_z * n_y
    chunk = seg

    def rows_at(off, n):
        return pl.ds(pl.multiple_of(off, 8), n)

    def grad_copies(g, stage):
        def copy(src, dst, k, other):
            return pltpu.make_async_remote_copy(
                src_ref=src, dst_ref=dst, send_sem=gs.at[g, stage, k],
                recv_sem=gr.at[g, stage, k], device_id=other, device_id_type=MESH,
            )

        off_c = core * len_c
        off_y = off_c + row_y * len_y
        off_z = off_y + pos_z * len_z
        out = []
        if stage == 0:
            out.append(copy(GA.at[g, rows_at((1 - core) * len_c, len_c)], GC.at[g], 0, partner))
        if stage == 1:
            for j in range(1, n_y):
                part = GB.at[g, rows_at(((row_y + j) % n_y) * len_y, len_y)]
                out.append(copy(part, GY.at[g, j - 1], j - 1, grad_y(j)))
        if stage == 2:
            for j in range(1, n_z):
                part = GD.at[g, rows_at(((pos_z + j) % n_z) * len_z, len_z)]
                out.append(copy(part, GZ.at[g, j - 1], j - 1, grad_z(j)))
        if stage == 3:
            for j in range(1, NGY):
                out.append(copy(GE.at[g], GX.at[g, gy], j - 1, peer_y(j)))
        if stage == 4:
            for j in range(1, n_z):
                part = GF.at[g, rows_at(off_z, len_z)]
                out.append(copy(part, part, j - 1, grad_z(j)))
        if stage == 5:
            for j in range(1, n_y):
                part = GF.at[g, rows_at(off_y, len_y)]
                out.append(copy(part, part, j - 1, grad_y(j)))
        if stage == 6:
            part = GF.at[g, rows_at(off_c, len_c)]
            out.append(copy(part, part, 0, partner))
        return out

    def grad_step(g, stage):
        if stage > 0:
            wait_all(grad_copies(g, stage - 1))
        if stage == 1:
            def fold(i, carry):
                at = rows_at(i * chunk, chunk)
                GB[g, at] = GA[g, rows_at(core * len_c + i * chunk, chunk)] + GC[g, at]
                return carry

            lax.fori_loop(0, len_c // chunk, fold, 0)
        if stage == 2:
            def fold(i, carry):
                at = rows_at(i * chunk, chunk)
                v = GB[g, rows_at(row_y * len_y + i * chunk, chunk)]
                for j in range(n_y - 1):
                    v = v + GY[g, j, at]
                GD[g, at] = v
                return carry

            lax.fori_loop(0, len_y // chunk, fold, 0)
        if stage == 3:
            v = GD[g, rows_at(pos_z * len_z, len_z)]
            for j in range(n_z - 1):
                v = v + GZ[g, j]
            GE[g] = v
            GX[g, gy] = v
        if stage == 4:
            v = GX[g, 0]
            for j in range(1, NGY):
                v = v + GX[g, j]
            GF[g, rows_at(core * len_c + row_y * len_y + pos_z * len_z, len_z)] = v
        if stage < 7:
            start_all(grad_copies(g, stage))

    total_cells = X * NGX * Y * NGY * Z * NGZ
    scale = 1.0 / math.sqrt(total_cells / 8.0)

    def grad_store(g, out_ref):
        def one(t, carry):
            out_ref[t] = GF[g, rows_at(t * C, C)][:, 0:C] * scale
            return carry

        lax.fori_loop(0, 27, one, 0)

    start_all(plane_copies(0, S))
    start_all(plane_copies(1, CT))

    def load_weights(t, carry):
        at = pl.ds(pl.multiple_of(t * L, L), C)
        whole = pl.ds(pl.multiple_of(t * L, L), L)
        W1[at, 0:C] = w1_ref[t]
        W2[at, 0:C] = w2_ref[t]
        back = pl.ds(pl.multiple_of((t - t % 3 + 2 - t % 3) * L, L), L)
        T1[back, :] = W1[whole, :].T
        T2[back, :] = W2[whole, :].T
        return carry

    lax.fori_loop(0, 27, load_weights, 0)

    wait_all(plane_copies(0, S))
    send_faces(0, S)
    wait_all(face_copies(0))

    at_y = lax.broadcasted_iota(jnp.int32, (YE, L), 0)
    live_y = jnp.where(
        ((at_y == 0) & (gy == 0)) | ((at_y == YE - 1) & (gy == NGY - 1)), 0.0, 1.0
    ).astype(F32)
    live_z = [jnp.where(gz == 0, 0.0, 1.0), jnp.where(gz == NGZ - 1, 0.0, 1.0)]

    def spread_lanes(v):
        return jnp.broadcast_to(v[..., L - 1 : L], v.shape)

    def first_input(x, carry):
        gone = ((x == 0) & (gx == 0)) | ((x == XE - 1) & (gx == NGX - 1))
        live = live_y * jnp.where(gone, 0.0, 1.0)
        s = S[x]
        m = spread_lanes(s) * live[:, None, :]
        MK[x] = m
        s = s * m
        S[x] = s
        faces = []
        for k in range(2):
            f = ZR[0, k, x]
            mf = spread_lanes(f) * (live * live_z[k])
            MZ[k, x] = mf
            f = f * mf
            ZR[0, k, x] = f
            faces.append(f)
        put(PS, x, s, faces[0], faces[1])
        return carry

    lax.fori_loop(0, XE, first_input, 0)

    def keep_y1(h, y):
        Y1[pl.ds(1 + h * H, H), 1 : 1 + Y, :, :] = y * own(MK, h)

    convolve(PS, W1, False, keep_y1)

    def norm_begin(k, ref):
        first, count = local_sum(lambda x: (mid(ref, x), mid(MK, x)))
        mean = first / jnp.maximum(count, 1.0)

        def deviation(x):
            d = (mid(ref, x) - mean) * mid(MK, x)
            return (d * d,)

        (second,) = local_sum(deviation)
        return [first, second, count]

    def norm_exchange(k, q, ref):
        rows = norm_begin(k, ref)
        sum_start(k, 0, rows)
        start_all(plane_copies(q, ref))
        rows = sum_wait(k, 0, True)
        sum_start(k, 1, rows)
        wait_all(plane_copies(q, ref))
        send_faces(q, ref)
        rows = sum_wait(k, 1, True)
        sum_start(k, 2, rows)
        wait_all(face_copies(q))
        rows = sum_wait(k, 2, True)
        mean = rows[0] / rows[2]
        rstd = lax.rsqrt(rows[1] / rows[2] + 1e-05)
        return mean, rstd, rows[2]

    mean1, rstd1, count = norm_exchange(0, 2, Y1)
    gain1, gain2, shift1, shift2 = GS[0:1], GS[1:2], GS[2:3], GS[3:4]

    def second_input(x, carry):
        def act(y, m):
            n = (y - mean1) * rstd1
            pre = gain1 * n + shift1
            return n, m * (pre * sigmoid(pre))

        n, hidden = act(Y1[x], MK[x])
        N1[x] = n
        faces = []
        for k in range(2):
            nf, hf = act(ZR[2, k, x], MZ[k, x])
            NZ1[k, x] = nf
            faces.append(hf)
        put(PH, x, hidden, faces[0], faces[1])
        return carry

    lax.fori_loop(0, XE, second_input, 0)

    def keep_y2(h, y):
        Y2[pl.ds(1 + h * H, H), 1 : 1 + Y, :, :] = y * own(MK, h)

    convolve(PH, W2, False, keep_y2)
    wait_all(plane_copies(1, CT))
    send_faces(1, CT)
    mean2, rstd2, _ = norm_exchange(1, 3, Y2)
    wait_all(face_copies(1))

    def outgoing(y, s, m, ct):
        n = (y - mean2) * rstd2
        pre = gain2 * n + shift2 + s
        sig = sigmoid(pre)
        return n, m * (pre * sig), ct * m * (sig * (1.0 + pre * (1.0 - sig)))

    lane = lax.broadcasted_iota(jnp.int32, (1, L), 1)
    inner = jnp.where(lane < C, 1.0, 0.0).astype(F32)

    def last_forward(x, carry):
        n, out, d = outgoing(Y2[x], S[x] * inner, MK[x], CT[x])
        N2[x] = n
        D2[x] = d

        @pl.when((x >= 1) & (x <= X))
        def _():
            result_ref[x - 1] = out[1 : 1 + Y, :, 0:C].astype(BF16)

        for k in range(2):
            nf, _, df = outgoing(ZR[3, k, x], ZR[0, k, x] * inner, MZ[k, x], ZR[1, k, x])
            NZ2[k, x] = nf
            DZ2[k, x] = df
        return carry

    lax.fori_loop(0, XE, last_forward, 0)

    rows = local_sum(lambda x: (mid(D2, x), mid(D2, x) * mid(N2, x)))
    for axis in range(3):
        sum_start(2, axis, rows)
        rows = sum_wait(2, axis, False)
    sum2, cross2 = rows

    def third_input(x, carry):
        factor = gain2 * rstd2

        def back(d, n, m):
            return m * factor * (d - sum2 / count - n * cross2 / count)

        main = back(D2[x], N2[x], MK[x])
        faces = [back(DZ2[k, x], NZ2[k, x], MZ[k, x]) for k in range(2)]
        put(PD2, x, main, faces[0], faces[1])
        return carry

    lax.fori_loop(0, XE, third_input, 0)

    def keep_d1(h, v):
        pre = gain1 * own(N1, h) + shift1
        sig = sigmoid(pre)
        D1[pl.ds(1 + h * H, H), 1 : 1 + Y, :, :] = (
            v * own(MK, h) * (sig * (1.0 + pre * (1.0 - sig)))
        )

    convolve(PD2, T2, True, keep_d1)
    rows = local_sum(lambda x: (mid(D1, x), mid(D1, x) * mid(N1, x)))
    sum_start(3, 0, rows)
    start_all(plane_copies(4, D1))
    products(1, PH, PD2)
    grad_step(1, 0)
    rows = sum_wait(3, 0, False)
    sum_start(3, 1, rows)
    wait_all(plane_copies(4, D1))
    send_faces(4, D1)
    rows = sum_wait(3, 1, False)
    sum_start(3, 2, rows)
    grad_step(1, 1)
    wait_all(face_copies(4))
    sum1, cross1 = sum_wait(3, 2, False)

    def fourth_input(x, carry):
        factor = gain1 * rstd1

        def back(d, n, m):
            return m * factor * (d - sum1 / count - n * cross1 / count)

        main = back(D1[x], N1[x], MK[x])
        faces = [back(ZR[4, k, x], NZ1[k, x], MZ[k, x]) for k in range(2)]
        put(PD1, x, main, faces[0], faces[1])
        return carry

    lax.fori_loop(0, XE, fourth_input, 0)
    products(0, PS, PD1)
    grad_step(0, 0)
    grad_step(1, 2)

    def keep_features(h, v):
        out = own(MK, h) * (own(D2, h) + v)
        gfeat_ref[pl.ds(h * H, H)] = out[:, :, :, 0:C].astype(BF16)

    convolve(PD1, T1, True, keep_features)
    at8 = lax.broadcasted_iota(jnp.int32, (8, L), 0)
    table = jnp.zeros((8, L), F32)
    for i, row in enumerate((cross1, sum1, cross2, sum2)):
        table = jnp.where(at8 == i, jnp.broadcast_to(row * scale, (8, L)), table)
    norm_ref[...] = table[0:4, 0:C]

    for stage in range(1, 8):
        grad_step(0, stage)
        if stage + 2 < 8:
            grad_step(1, stage + 2)
        if stage == 6:
            grad_store(1, g2_ref)
    grad_store(0, g1_ref)


def local(sizes, features, ground, thickness, weight_one, weight_two, gains, shifts, cotangent):
    NGX, NGY, NGZ = sizes
    X, Y, Z, C = features.shape
    n_y, n_z = NGZ // 2, NGX
    parts = 2 * n_y * n_z
    seg = -(-27 * C // (parts * 8)) * 8
    dims = (NGX, NGY, NGZ, X, Y, Z, C, seg)
    XE, YE = X + 2, Y + 2
    ext = pltpu.VMEM((XE, YE, Z, L), F32)
    face = pltpu.VMEM((2, XE, YE, L), F32)
    patch = pltpu.VMEM((XE, YE, Z, 3 * L), BF16)
    weights = pltpu.VMEM((27 * L, L), BF16)
    dma = pltpu.SemaphoreType.DMA
    scratch = [ext] * 9
    scratch += [pltpu.VMEM((5, 2, XE, YE, L), F32)] * 2
    scratch += [face] * 4
    scratch += [pltpu.VMEM((YE, Z + 16, L), F32)]
    scratch += [patch] * 4
    scratch += [pltpu.VMEM((L, X * Y * Z), BF16)]
    scratch += [weights] * 4
    scratch += [pltpu.VMEM((8, L), F32)]
    scratch += [pltpu.VMEM((4, 3, 8, L), F32)]
    scratch += [pltpu.VMEM((4, n, 8, L), F32) for n in (NGX, NGY, NGZ)]
    len_y, len_c = seg * n_z, seg * n_z * n_y
    scratch += [
        pltpu.VMEM((2, 2 * len_c, L), F32),
        pltpu.VMEM((2, len_c, L), F32),
        pltpu.VMEM((2, len_c, L), F32),
        pltpu.VMEM((2, max(n_y - 1, 1), len_y, L), F32),
        pltpu.VMEM((2, len_y, L), F32),
        pltpu.VMEM((2, n_z - 1, seg, L), F32),
        pltpu.VMEM((2, seg, L), F32),
        pltpu.VMEM((2, NGY, seg, L), F32),
        pltpu.VMEM((2, 2 * len_c, L), F32),
    ]
    sums = NGX + NGY + NGZ
    scratch += [dma((5, 8)), dma((5, 8)), dma((5, 2)), dma((5, 2))]
    scratch += [dma((4, sums)), dma((4, sums))]
    most = max(n_y, n_z, NGY) - 1
    scratch += [dma((2, 7, most)), dma((2, 7, most))]
    vmem = pl.BlockSpec(memory_space=pltpu.VMEM)
    smem = pl.BlockSpec(memory_space=pltpu.SMEM)
    return pl.pallas_call(
        functools.partial(body, dims),
        out_shape=(
            jax.ShapeDtypeStruct((X, Y, Z, C), BF16),
            jax.ShapeDtypeStruct((X, Y, Z, C), BF16),
            jax.ShapeDtypeStruct((27, C, C), F32),
            jax.ShapeDtypeStruct((27, C, C), F32),
            jax.ShapeDtypeStruct((4, C), F32),
        ),
        in_specs=[vmem, smem, smem, vmem, vmem, vmem, vmem, vmem],
        out_specs=(vmem,) * 5,
        scratch_shapes=scratch,
        compiler_params=pltpu.CompilerParams(
            collective_id=0, has_side_effects=True, vmem_limit_bytes=62 * 1024 * 1024
        ),
    )(features, ground, thickness, weight_one, weight_two, gains, shifts, cotangent)


def solution(mesh):
    sizes = tuple(mesh.shape[a] for a in ("gx", "gy", "gz"))
    return jax.shard_map(
        functools.partial(local, sizes),
        mesh=mesh,
        in_specs=(
            P("gx", "gy", "gz", None),
            P("gx", "gy"),
            P("gx", "gy"),
            P(),
            P(),
            P(),
            P(),
            P("gx", "gy", "gz", None),
        ),
        out_specs=(P("gx", "gy", "gz", None), P("gx", "gy", "gz", None), P(), P(), P()),
        check_vma=False,
    )
```

time: 1090 us -> 134 us (0.12); the launches traced: 1080 us -> 134 us
  blocking collectives: 449 us -> 0 us
  waiting for transfers between devices: 284 us -> 0 us
  Pallas kernels: 0 us -> 125 us
  local copies, waits for them, and re-layouts: 118 us -> 7.56 us
  starting transfers between devices: 87.7 us -> 0 us
  other arithmetic: 62.7 us -> 0 us
  matrix products: 60 us -> 0 us
  between operations: 16.5 us -> 0.65 us
    psum x6 -> x0, blocking collectives: 385 us -> none  [the longest x2 130 us: moments(): lax.psum((jnp.sum(values, axis=0), jnp.sum(mask_flat)), ('gx', 'gy', 'gz'))]
    psum x1 -> x0, waiting for transfers between devices: 164 us -> none  [local(): grad_w1, grad_w2 = lax.psum((grad_w1, grad_w2), ('gx', 'gy', 'gz'))]
    pallas_call x0 -> x1, Pallas kernels: none -> 125 us  [local(): pl.pallas_call(functools.partial(body, dims), out_shape=(jax.ShapeDtypeSt...]
    all_to_all x6 -> x0, waiting for transfers between devices: 85.7 us -> none  [the longest x3 51.3 us: dispatch(): lax.all_to_all(outgoing, 'gz', split_axis=0, concat_axis=0, tiled=True)]
    dot_general x54 -> x0, matrix products: 60 us -> none  [the longest x36 44.9 us: convolve(): jnp.dot(patch, stacked[row_off, col_off], preferred_element_type=jnp.floa...]
    ppermute x24 -> x0, starting transfers between devices: 58.2 us -> none  [the longest x12 37.7 us: with_halo(): lax.ppermute(lax.slice_in_dim(block, block.shape[dim] - width, None, axis...]
    unnamed x189 -> x9, local copies, waits for them, and re-layouts: 62.3 us -> 7.56 us
    all_to_all x2 -> x0, blocking collectives: 53.5 us -> none  [the longest x1 28.9 us: collect(): lax.all_to_all(leaving, 'gz', split_axis=0, concat_axis=0, tiled=True)]
  transfers between devices with their start and end apart: 31 -> 0, of which waited for: 18 -> 0; matrix products, arithmetic and copies ran while one was open for 5% -> 0% of each run, Pallas kernels for 0% -> 0%
where the time goes in v1:
time: 134 us
  Pallas kernels  125 us (93%)
  local copies, waits for them, and re-layouts  7.56 us (6%)
    pallas_call x1, Pallas kernels, local(): pl.pallas_call(functools.partial(body, dims), out_shape=(jax.ShapeDtypeSt...  125 us
    unnamed x9, local copies, waits for them, and re-layouts  7.56 us

profile of v1, /device:TPU:1, one launch (start us, length us, event | category | flops | bytes accessed | tf_op | source)
XLA Modules:
  0.0 133.7 jit_solution(18039656586136599139)
XLA Ops:
  0.6 125.5 %shard_map.119 = (bf16[8,8,16,96]{3,2,1,0:T(8,128)(2,1)}, bf16[8,8,16,96]{3,2,1,0:T(8,128)(2,1)}, f32[27,96,96]{2,1,0:T(8,128)}, f32[27,96,96]{2,1,0:T(8,128)}, f32[4,96]{1,0:T(4,128)}) custom-call(bf16[8,8,16,96]{3,2,1,0:T(8,128)(2,1)} %feat_ref.1, s32[8,8]{1,0:T(8,128)} %ground_ref.1, s32[8,8]{1,0:T(8,128)} %thick_ref.1, bf16[27,96,96]{2,1,0:T(8,128)(2,1)} %w1_ref.1, ...), custom_call_target="tpu_custom_call" | custom-call | tf_op jit(solution)/shard_map/pallas_call | solution.py:603
  126.1 1.7 %copy.18 = bf16[8,8,16,96]{3,2,1,0:T(8,128)(2,1)} copy(bf16[8,8,16,96]{3,2,1,0:T(8,128)(2,1)} %get-tuple-element.10) | data formatting | bytes 393216
  127.8 1.7 %copy.19 = bf16[8,8,16,96]{3,2,1,0:T(8,128)(2,1)} copy(bf16[8,8,16,96]{3,2,1,0:T(8,128)(2,1)} %get-tuple-element.11) | data formatting | bytes 393216
  129.5 0.0 copy-start
  129.5 2.6 %copy.20 = f32[27,96,96]{2,1,0:T(8,128)} copy(f32[27,96,96]{2,1,0:T(8,128)} %get-tuple-element.12) | data formatting | bytes 1990656
  132.0 0.0 copy-done
  132.0 0.0 copy-start.1
  132.1 1.1 copy.21
  133.1 0.0 copy-done.1
  133.1 0.6 copy.22
Async XLA Ops:
  129.5 2.6 %copy-start = (f32[27,96,96]{2,1,0:T(8,128)S(1)}, f32[27,96,96]{2,1,0:T(8,128)}, u32[]{:S(2)}) copy-start(f32[27,96,96]{2,1,0:T(8,128)} %get-tuple-element.13) | copy-start | bytes 2985988
  132.0 1.1 copy-start.1

commit v2 on v1

--- a/solution.py
+++ b/solution.py
@@ -21,16 +21,19 @@
 
 def body(
     dims,
-    feat_ref, ground_ref, thick_ref, w1_ref, w2_ref, gains_ref, shifts_ref, cot_ref,
+    feat_in, ground_in, thick_in, w1_in, w2_in, gains_in, shifts_in, cot_in,
+    result_out, gfeat_out, g1_out, g2_out, norm_out,
+    feat_ref, cot_ref, w1_ref, w2_ref, gains_ref, shifts_ref, ground_ref, thick_ref,
     result_ref, gfeat_ref, g1_ref, g2_ref, norm_ref,
     S, CT, Y1, Y2, D1, MK, N1, N2, D2,
     ZS, ZR, MZ, NZ1, NZ2, DZ2,
     V, PS, PH, PD2, PD1, DT, W1, W2, T1, T2, GS,
-    STS, RX, RY, RZ,
-    GA, GC, GB, GY, GD, GZ, GE, GX, GF,
-    hs, hr, zs, zr, ss, sr, gs, gr,
+    STS, RA, RB,
+    GA, GC, GF, *rest,
 ):
-    NGX, NGY, NGZ, X, Y, Z, C, seg = dims
+    NGX, NGY, NGZ, X, Y, Z, C, segs = dims
+    portions = [rest[6 * p : 6 * p + 6] for p in range(3)]
+    hs, hr, zs, zr, ss, sr, gs, gr, ins, outs = rest[18:]
     XE, YE = X + 2, Y + 2
     gx, gy, gz = lax.axis_index("gx"), lax.axis_index("gy"), lax.axis_index("gz")
     nz_lo, n_y = NGX // 2, NGZ // 2
@@ -42,14 +45,8 @@
     def dev(ax, ay, az):
         return (ax, ay, az)
 
-    def peer_x(j):
-        return dev((gx + j) % NGX, gy, gz)
-
     def peer_y(j):
         return dev(gx, (gy + j) % NGY, gz)
-
-    def peer_z(j):
-        return dev(gx, gy, (gz + j) % NGZ)
 
     def side(dx, dy):
         return dev((gx + dx + NGX) % NGX, (gy + dy + NGY) % NGY, gz)
@@ -62,20 +59,46 @@
         return dev((other % nz_lo) * 2 + core, gy, row_y * 2 + other // nz_lo)
 
     partner = dev(z_lo * 2 + 1 - core, gy, gz)
-
-    greet = [peer_x(j) for j in range(1, NGX)]
-    greet += [peer_y(j) for j in range(1, NGY)]
-    greet += [peer_z(j) for j in range(1, NGZ)]
-    greet += [side(dx, dy) for dx, dy in SIDES if dx and dy]
-    greet += [grad_z(j) for j in range(1, n_z)]
+    n_a, n_b = 2 * n_z, NGY * n_y
+    me_a, me_b = pos_z * 2 + core, gy * n_y + row_y
+
+    def peer_a(j):
+        other = (me_a + j) % n_a
+        pos = other // 2
+        return dev((pos % nz_lo) * 2 + other % 2, gy, row_y * 2 + pos // nz_lo)
+
+    def peer_b(j):
+        other = (me_b + j) % n_b
+        return dev(gx, other // n_y, (other % n_y) * 2 + z_hi)
+
+    down = dev(gx, gy, (gz + NGZ - 1) % NGZ)
+    up = dev(gx, gy, (gz + 1) % NGZ)
+
+    greet = [peer_a(j) for j in range(1, n_a)]
+    greet += [peer_b(j) for j in range(1, n_b)]
+    greet += [down, up]
+    greet += [side(dx, dy) for dx, dy in SIDES]
     barrier = pltpu.get_barrier_semaphore()
     for other in greet:
         pl.semaphore_signal(barrier, inc=1, device_id=other, device_id_type=MESH)
 
+    arrivals = [
+        pltpu.make_async_copy(src, dst, ins.at[i])
+        for i, (src, dst) in enumerate(
+            (
+                (ground_in, ground_ref), (thick_in, thick_ref), (feat_in, feat_ref),
+                (cot_in, cot_ref), (w1_in, w1_ref), (gains_in, gains_ref),
+                (shifts_in, shifts_ref), (w2_in, w2_ref),
+            )
+        )
+    ]
+    for c in arrivals:
+        c.start()
+
     for ref in (W1, W2, T1, T2, GS):
         ref[...] = jnp.zeros(ref.shape, ref.dtype)
-    GS[0:2, 0:C] = gains_ref[...]
-    GS[2:4, 0:C] = shifts_ref[...]
+    for c in arrivals[:4]:
+        c.wait()
 
     def load_block(x, carry):
         level = lax.broadcasted_iota(jnp.int32, (Z, L), 0) + gz * Z
@@ -115,8 +138,6 @@
         return out
 
     def face_copies(q):
-        down = dev(gx, gy, (gz + NGZ - 1) % NGZ)
-        up = dev(gx, gy, (gz + 1) % NGZ)
         out = []
         for k, other in ((0, down), (1, up)):
             out.append(
@@ -148,50 +169,42 @@
         lax.fori_loop(0, XE, one, 0)
         start_all(face_copies(q))
 
-    def sum_copies(k, axis):
-        n, me, peer, land = (
-            (NGX, gx, peer_x, RX), (NGY, gy, peer_y, RY), (NGZ, gz, peer_z, RZ)
-        )[axis]
-        base = (0, NGX, NGX + NGY)[axis]
-        out = []
-        for j in range(1, n):
-            out.append(
-                pltpu.make_async_remote_copy(
-                    src_ref=STS.at[k, axis],
-                    dst_ref=land.at[k, me],
-                    send_sem=ss.at[k, base + j],
-                    recv_sem=sr.at[k, base + j],
-                    device_id=peer(j),
-                    device_id_type=MESH,
-                )
+    def sum_copies(k, part):
+        n, me, peer, land = ((n_a, me_a, peer_a, RA), (n_b, me_b, peer_b, RB))[part]
+        base = (0, n_a)[part]
+        return [
+            pltpu.make_async_remote_copy(
+                src_ref=STS.at[k, part],
+                dst_ref=land.at[k, me],
+                send_sem=ss.at[base + j],
+                recv_sem=sr.at[k, base + j],
+                device_id=peer(j),
+                device_id_type=MESH,
             )
-        return out
-
-    def sum_start(k, axis, rows):
-        at = lax.broadcasted_iota(jnp.int32, (8, L), 0)
-        tile = jnp.zeros((8, L), F32)
+            for j in range(1, n)
+        ]
+
+    def sum_start(k, part, rows):
+        at = lax.broadcasted_iota(jnp.int32, (4, L), 0)
+        tile = jnp.zeros((4, L), F32)
         for i, row in enumerate(rows):
-            tile = jnp.where(at == i, jnp.broadcast_to(row, (8, L)), tile)
-        STS[k, axis] = tile
-        me, land = ((gx, RX), (gy, RY), (gz, RZ))[axis]
+            tile = jnp.where(at == i, jnp.broadcast_to(row, (4, L)), tile)
+        STS[k, part] = tile
+        me, land = ((me_a, RA), (me_b, RB))[part]
         land[k, me] = tile
-        start_all(sum_copies(k, axis))
-
-    def sum_wait(k, axis, spread):
-        n, land = ((NGX, RX), (NGY, RY), (NGZ, RZ))[axis]
-        wait_all(sum_copies(k, axis))
-        tiles = [land[k, i] for i in range(n)]
-        rows = [[t[i : i + 1] for t in tiles] for i in range(3)]
-        first = functools.reduce(jnp.add, rows[0])
-        second = functools.reduce(jnp.add, rows[1])
+        start_all(sum_copies(k, part))
+
+    def sum_wait(k, part, spread):
+        n, land = ((n_a, RA), (n_b, RB))[part]
+        wait_all(sum_copies(k, part))
+        tiles = land[k]
+        first, second, third = (jnp.sum(tiles[:, i], axis=0, keepdims=True) for i in range(3))
         if not spread:
             return [first, second]
-        count = functools.reduce(jnp.add, rows[2])
-        mean = first / jnp.maximum(count, 1.0)
-        for s, m in zip(rows[0], rows[2]):
-            off = s / jnp.maximum(m, 1.0) - mean
-            second = second + m * off * off
-        return [first, second, count]
+        mean = first / jnp.maximum(third, 1.0)
+        each = tiles[:, 0] / jnp.maximum(tiles[:, 2], 1.0) - mean
+        second = second + jnp.sum(tiles[:, 2] * each * each, axis=0, keepdims=True)
+        return [first, second, third]
 
     def put(dest, x, main, low, high):
         V[:, 8 : 8 + Z, :] = main
@@ -238,10 +251,11 @@
     def mid(ref, x):
         return ref[x, 1 : 1 + Y, :, :]
 
-    def products(g, src, dy):
+    def prepare(dy):
         flat = dy[1 : 1 + X, 1 : 1 + Y, :, L : 2 * L].reshape(X * Y * Z, L)
         DT[...] = flat.T
 
+    def products(g, src, first, last):
         def one(k, carry):
             a, b = k // 3, k % 3
             patch = src[pl.ds(a, X), pl.ds(b, Y), :, :].reshape(X * Y * Z, 3 * L)
@@ -252,15 +266,22 @@
                 )
             return carry
 
-        lax.fori_loop(0, 9, one, 0)
-
-    len_z = seg
-    len_y = seg * n_z
-    len_c = seg * n_z * n_y
-    chunk = seg
+        lax.fori_loop(first, last, one, 0)
+
+    axes = ((n_y, row_y, grad_y), (n_z, pos_z, grad_z), (NGY, gy, peer_y))
+    plans = []
+    base = 0
+    for p in range(3):
+        plan = [axes[(p + i) % 3] for i in range(3)]
+        len1 = plan[1][0] * segs[p]
+        plans.append((plan, base, len1, segs[p]))
+        base += plan[0][0] * len1
+    len_c = base
 
     def rows_at(off, n):
         return pl.ds(pl.multiple_of(off, 8), n)
+
+    most = max(n_y, n_z, NGY) - 1
 
     def grad_copies(g, stage):
         def copy(src, dst, k, other):
@@ -269,67 +290,64 @@
                 recv_sem=gr.at[g, stage, k], device_id=other, device_id_type=MESH,
             )
 
-        off_c = core * len_c
-        off_y = off_c + row_y * len_y
-        off_z = off_y + pos_z * len_z
+        if stage == 0:
+            return [copy(GA.at[g, rows_at((1 - core) * len_c, len_c)], GC.at[g], 0, partner)]
+        if stage == 6:
+            part = GF.at[g, rows_at(core * len_c, len_c)]
+            return [copy(part, part, 0, partner)]
         out = []
-        if stage == 0:
-            out.append(copy(GA.at[g, rows_at((1 - core) * len_c, len_c)], GC.at[g], 0, partner))
-        if stage == 1:
-            for j in range(1, n_y):
-                part = GB.at[g, rows_at(((row_y + j) % n_y) * len_y, len_y)]
-                out.append(copy(part, GY.at[g, j - 1], j - 1, grad_y(j)))
-        if stage == 2:
-            for j in range(1, n_z):
-                part = GD.at[g, rows_at(((pos_z + j) % n_z) * len_z, len_z)]
-                out.append(copy(part, GZ.at[g, j - 1], j - 1, grad_z(j)))
-        if stage == 3:
-            for j in range(1, NGY):
-                out.append(copy(GE.at[g], GX.at[g, gy], j - 1, peer_y(j)))
-        if stage == 4:
-            for j in range(1, n_z):
-                part = GF.at[g, rows_at(off_z, len_z)]
-                out.append(copy(part, part, j - 1, grad_z(j)))
-        if stage == 5:
-            for j in range(1, n_y):
-                part = GF.at[g, rows_at(off_y, len_y)]
-                out.append(copy(part, part, j - 1, grad_y(j)))
-        if stage == 6:
-            part = GF.at[g, rows_at(off_c, len_c)]
-            out.append(copy(part, part, 0, partner))
+        for p, (plan, base, len1, seg) in enumerate(plans):
+            GB, GY, GD, GZ, GE, GX = portions[p]
+            n, me, peer = plan[(None, 0, 1, 2, 1, 0)[stage]]
+            off1 = core * len_c + base + plan[0][1] * len1
+            off2 = off1 + plan[1][1] * seg
+            for j in range(1, n):
+                if stage == 1:
+                    part = GB.at[g, rows_at(((me + j) % n) * len1, len1)]
+                    land = GY.at[g, j - 1]
+                elif stage == 2:
+                    part = GD.at[g, rows_at(((me + j) % n) * seg, seg)]
+                    land = GZ.at[g, j - 1]
+                elif stage == 3:
+                    part, land = GE.at[g], GX.at[g, me]
+                elif stage == 4:
+                    part = land = GF.at[g, rows_at(off2, seg)]
+                else:
+                    part = land = GF.at[g, rows_at(off1, len1)]
+                out.append(copy(part, land, p * most + j - 1, peer(j)))
         return out
 
     def grad_step(g, stage):
         if stage > 0:
             wait_all(grad_copies(g, stage - 1))
-        if stage == 1:
-            def fold(i, carry):
-                at = rows_at(i * chunk, chunk)
-                GB[g, at] = GA[g, rows_at(core * len_c + i * chunk, chunk)] + GC[g, at]
-                return carry
-
-            lax.fori_loop(0, len_c // chunk, fold, 0)
-        if stage == 2:
-            def fold(i, carry):
-                at = rows_at(i * chunk, chunk)
-                v = GB[g, rows_at(row_y * len_y + i * chunk, chunk)]
-                for j in range(n_y - 1):
-                    v = v + GY[g, j, at]
-                GD[g, at] = v
-                return carry
-
-            lax.fori_loop(0, len_y // chunk, fold, 0)
-        if stage == 3:
-            v = GD[g, rows_at(pos_z * len_z, len_z)]
-            for j in range(n_z - 1):
-                v = v + GZ[g, j]
-            GE[g] = v
-            GX[g, gy] = v
-        if stage == 4:
-            v = GX[g, 0]
-            for j in range(1, NGY):
-                v = v + GX[g, j]
-            GF[g, rows_at(core * len_c + row_y * len_y + pos_z * len_z, len_z)] = v
+        for p, (plan, base, len1, seg) in enumerate(plans):
+            GB, GY, GD, GZ, GE, GX = portions[p]
+            if stage == 1:
+                def fold(i, carry):
+                    at = i * len1 + base
+                    GB[g, rows_at(i * len1, len1)] = (
+                        GA[g, rows_at(core * len_c + at, len1)] + GC[g, rows_at(at, len1)]
+                    )
+                    return carry
+
+                lax.fori_loop(0, plan[0][0], fold, 0)
+            if stage == 2:
+                v = GB[g, rows_at(plan[0][1] * len1, len1)]
+                for j in range(plan[0][0] - 1):
+                    v = v + GY[g, j]
+                GD[g] = v
+            if stage == 3:
+                v = GD[g, rows_at(plan[1][1] * seg, seg)]
+                for j in range(plan[1][0] - 1):
+                    v = v + GZ[g, j]
+                GE[g] = v
+                GX[g, plan[2][1]] = v
+            if stage == 4:
+                v = GX[g, 0]
+                for j in range(1, plan[2][0]):
+                    v = v + GX[g, j]
+                off = core * len_c + base + plan[0][1] * len1 + plan[1][1] * seg
+                GF[g, rows_at(off, seg)] = v
         if stage < 7:
             start_all(grad_copies(g, stage))
 
@@ -344,23 +362,33 @@
         lax.fori_loop(0, 27, one, 0)
 
     start_all(plane_copies(0, S))
-    start_all(plane_copies(1, CT))
-
-    def load_weights(t, carry):
-        at = pl.ds(pl.multiple_of(t * L, L), C)
+    for c in arrivals[4:7]:
+        c.wait()
+    GS[0:2, 0:C] = gains_ref[...]
+    GS[2:4, 0:C] = shifts_ref[...]
+
+    def load_first(t, carry):
+        W1[pl.ds(pl.multiple_of(t * L, L), C), 0:C] = w1_ref[t]
+        return carry
+
+    lax.fori_loop(0, 27, load_first, 0)
+
+    def load_rest(t, carry):
+        W2[pl.ds(pl.multiple_of(t * L, L), C), 0:C] = w2_ref[t]
         whole = pl.ds(pl.multiple_of(t * L, L), L)
-        W1[at, 0:C] = w1_ref[t]
-        W2[at, 0:C] = w2_ref[t]
         back = pl.ds(pl.multiple_of((t - t % 3 + 2 - t % 3) * L, L), L)
         T1[back, :] = W1[whole, :].T
         T2[back, :] = W2[whole, :].T
         return carry
 
-    lax.fori_loop(0, 27, load_weights, 0)
+    def fill_weights():
+        arrivals[7].wait()
+        lax.fori_loop(0, 27, load_rest, 0)
 
     wait_all(plane_copies(0, S))
     send_faces(0, S)
     wait_all(face_copies(0))
+    start_all(plane_copies(1, CT))
 
     at_y = lax.broadcasted_iota(jnp.int32, (YE, L), 0)
     live_y = jnp.where(
@@ -408,7 +436,7 @@
         (second,) = local_sum(deviation)
         return [first, second, count]
 
-    def norm_exchange(k, q, ref):
+    def norm_exchange(k, q, ref, fill):
         rows = norm_begin(k, ref)
         sum_start(k, 0, rows)
         start_all(plane_copies(q, ref))
@@ -416,15 +444,16 @@
         sum_start(k, 1, rows)
         wait_all(plane_copies(q, ref))
         send_faces(q, ref)
+        fill()
+        wait_all(face_copies(q))
         rows = sum_wait(k, 1, True)
-        sum_start(k, 2, rows)
-        wait_all(face_copies(q))
-        rows = sum_wait(k, 2, True)
         mean = rows[0] / rows[2]
         rstd = lax.rsqrt(rows[1] / rows[2] + 1e-05)
         return mean, rstd, rows[2]
 
-    mean1, rstd1, count = norm_exchange(0, 2, Y1)
+    wait_all(plane_copies(1, CT))
+    send_faces(1, CT)
+    mean1, rstd1, count = norm_exchange(0, 2, Y1, fill_weights)
     gain1, gain2, shift1, shift2 = GS[0:1], GS[1:2], GS[2:3], GS[3:4]
 
     def second_input(x, carry):
@@ -449,10 +478,7 @@
         Y2[pl.ds(1 + h * H, H), 1 : 1 + Y, :, :] = y * own(MK, h)
 
     convolve(PH, W2, False, keep_y2)
-    wait_all(plane_copies(1, CT))
-    send_faces(1, CT)
-    mean2, rstd2, _ = norm_exchange(1, 3, Y2)
-    wait_all(face_copies(1))
+    mean2, rstd2, _ = norm_exchange(1, 3, Y2, lambda: wait_all(face_copies(1)))
 
     def outgoing(y, s, m, ct):
         n = (y - mean2) * rstd2
@@ -480,10 +506,13 @@
 
     lax.fori_loop(0, XE, last_forward, 0)
 
+    results = [pltpu.make_async_copy(result_ref, result_out, outs.at[0])]
+    results[0].start()
+
     rows = local_sum(lambda x: (mid(D2, x), mid(D2, x) * mid(N2, x)))
-    for axis in range(3):
-        sum_start(2, axis, rows)
-        rows = sum_wait(2, axis, False)
+    for part in range(2):
+        sum_start(2, part, rows)
+        rows = sum_wait(2, part, False)
     sum2, cross2 = rows
 
     def third_input(x, carry):
@@ -510,17 +539,16 @@
     rows = local_sum(lambda x: (mid(D1, x), mid(D1, x) * mid(N1, x)))
     sum_start(3, 0, rows)
     start_all(plane_copies(4, D1))
-    products(1, PH, PD2)
-    grad_step(1, 0)
+    prepare(PD2)
+    products(1, PH, 0, 3)
     rows = sum_wait(3, 0, False)
     sum_start(3, 1, rows)
     wait_all(plane_copies(4, D1))
     send_faces(4, D1)
-    rows = sum_wait(3, 1, False)
-    sum_start(3, 2, rows)
-    grad_step(1, 1)
+    products(1, PH, 3, 9)
+    grad_step(1, 0)
     wait_all(face_copies(4))
-    sum1, cross1 = sum_wait(3, 2, False)
+    sum1, cross1 = sum_wait(3, 1, False)
 
     def fourth_input(x, carry):
         factor = gain1 * rstd1
@@ -534,7 +562,9 @@
         return carry
 
     lax.fori_loop(0, XE, fourth_input, 0)
-    products(0, PS, PD1)
+    grad_step(1, 1)
+    prepare(PD1)
+    products(0, PS, 0, 9)
     grad_step(0, 0)
     grad_step(1, 2)
 
@@ -549,29 +579,57 @@
         table = jnp.where(at8 == i, jnp.broadcast_to(row * scale, (8, L)), table)
     norm_ref[...] = table[0:4, 0:C]
 
+    results.append(pltpu.make_async_copy(norm_ref, norm_out, outs.at[1]))
+    results.append(pltpu.make_async_copy(gfeat_ref, gfeat_out, outs.at[2]))
+    results[1].start()
+    results[2].start()
+
     for stage in range(1, 8):
         grad_step(0, stage)
         if stage + 2 < 8:
             grad_step(1, stage + 2)
         if stage == 6:
             grad_store(1, g2_ref)
+            results.append(pltpu.make_async_copy(g2_ref, g2_out, outs.at[3]))
+            results[3].start()
     grad_store(0, g1_ref)
+    results.append(pltpu.make_async_copy(g1_ref, g1_out, outs.at[4]))
+    results[4].start()
+    for c in results:
+        c.wait()
 
 
 def local(sizes, features, ground, thickness, weight_one, weight_two, gains, shifts, cotangent):
     NGX, NGY, NGZ = sizes
     X, Y, Z, C = features.shape
     n_y, n_z = NGZ // 2, NGX
-    parts = 2 * n_y * n_z
-    seg = -(-27 * C // (parts * 8)) * 8
-    dims = (NGX, NGY, NGZ, X, Y, Z, C, seg)
+    n = (n_y, n_z, NGY)
+    pairs = [n[p] * n[(p + 1) % 3] for p in range(3)]
+    tiles = -(-27 * C // (2 * 8 * min(pairs)))
+    segs = tuple(8 * (tiles // 3 + (p < tiles % 3)) for p in range(3))
+    dims = (NGX, NGY, NGZ, X, Y, Z, C, segs)
     XE, YE = X + 2, Y + 2
     ext = pltpu.VMEM((XE, YE, Z, L), F32)
     face = pltpu.VMEM((2, XE, YE, L), F32)
     patch = pltpu.VMEM((XE, YE, Z, 3 * L), BF16)
     weights = pltpu.VMEM((27 * L, L), BF16)
     dma = pltpu.SemaphoreType.DMA
-    scratch = [ext] * 9
+    scratch = [
+        pltpu.VMEM((X, Y, Z, C), BF16),
+        pltpu.VMEM((X, Y, Z, C), BF16),
+        pltpu.VMEM((27, C, C), BF16),
+        pltpu.VMEM((27, C, C), BF16),
+        pltpu.VMEM((2, C), F32),
+        pltpu.VMEM((2, C), F32),
+        pltpu.SMEM((X, Y), jnp.int32),
+        pltpu.SMEM((X, Y), jnp.int32),
+        pltpu.VMEM((X, Y, Z, C), BF16),
+        pltpu.VMEM((X, Y, Z, C), BF16),
+        pltpu.VMEM((27, C, C), F32),
+        pltpu.VMEM((27, C, C), F32),
+        pltpu.VMEM((4, C), F32),
+    ]
+    scratch += [ext] * 9
     scratch += [pltpu.VMEM((5, 2, XE, YE, L), F32)] * 2
     scratch += [face] * 4
     scratch += [pltpu.VMEM((YE, Z + 16, L), F32)]
@@ -579,27 +637,32 @@
     scratch += [pltpu.VMEM((L, X * Y * Z), BF16)]
     scratch += [weights] * 4
     scratch += [pltpu.VMEM((8, L), F32)]
-    scratch += [pltpu.VMEM((4, 3, 8, L), F32)]
-    scratch += [pltpu.VMEM((4, n, 8, L), F32) for n in (NGX, NGY, NGZ)]
-    len_y, len_c = seg * n_z, seg * n_z * n_y
+    n_a, n_b = 2 * n_z, NGY * n_y
+    scratch += [pltpu.VMEM((4, 2, 4, L), F32)]
+    scratch += [pltpu.VMEM((4, k, 4, L), F32) for k in (n_a, n_b)]
+    len_c = sum(a * b for a, b in zip(pairs, segs))
     scratch += [
         pltpu.VMEM((2, 2 * len_c, L), F32),
         pltpu.VMEM((2, len_c, L), F32),
-        pltpu.VMEM((2, len_c, L), F32),
-        pltpu.VMEM((2, max(n_y - 1, 1), len_y, L), F32),
-        pltpu.VMEM((2, len_y, L), F32),
-        pltpu.VMEM((2, n_z - 1, seg, L), F32),
-        pltpu.VMEM((2, seg, L), F32),
-        pltpu.VMEM((2, NGY, seg, L), F32),
         pltpu.VMEM((2, 2 * len_c, L), F32),
     ]
-    sums = NGX + NGY + NGZ
+    for p in range(3):
+        n1, n2, n3 = n[p], n[(p + 1) % 3], n[(p + 2) % 3]
+        seg = segs[p]
+        scratch += [
+            pltpu.VMEM((2, n1 * n2 * seg, L), F32),
+            pltpu.VMEM((2, n1 - 1, n2 * seg, L), F32),
+            pltpu.VMEM((2, n2 * seg, L), F32),
+            pltpu.VMEM((2, n2 - 1, seg, L), F32),
+            pltpu.VMEM((2, seg, L), F32),
+            pltpu.VMEM((2, n3, seg, L), F32),
+        ]
+    most = max(n) - 1
     scratch += [dma((5, 8)), dma((5, 8)), dma((5, 2)), dma((5, 2))]
-    scratch += [dma((4, sums)), dma((4, sums))]
-    most = max(n_y, n_z, NGY) - 1
-    scratch += [dma((2, 7, most)), dma((2, 7, most))]
-    vmem = pl.BlockSpec(memory_space=pltpu.VMEM)
-    smem = pl.BlockSpec(memory_space=pltpu.SMEM)
+    scratch += [dma((n_a + n_b,)), dma((4, n_a + n_b))]
+    scratch += [dma((2, 7, 3 * most)), dma((2, 7, 3 * most))]
+    scratch += [dma((8,)), dma((5,))]
+    anywhere = pl.BlockSpec(memory_space=pl.ANY)
     return pl.pallas_call(
         functools.partial(body, dims),
         out_shape=(
@@ -609,8 +672,8 @@
             jax.ShapeDtypeStruct((27, C, C), F32),
             jax.ShapeDtypeStruct((4, C), F32),
         ),
-        in_specs=[vmem, smem, smem, vmem, vmem, vmem, vmem, vmem],
-        out_specs=(vmem,) * 5,
+        in_specs=[anywhere] * 8,
+        out_specs=(anywhere,) * 5,
         scratch_shapes=scratch,
         compiler_params=pltpu.CompilerParams(
             collective_id=0, has_side_effects=True, vmem_limit_bytes=62 * 1024 * 1024

time: 134 us -> 114 us (0.85)
  Pallas kernels: 125 us -> 105 us
    pallas_call x1, Pallas kernels: 125 us -> 105 us  [local(): pl.pallas_call(functools.partial(body, dims), out_shape=(jax.ShapeDtypeSt...]
where the time goes in v2:
time: 114 us
  Pallas kernels  105 us (92%)
  local copies, waits for them, and re-layouts  7.56 us (7%)
    pallas_call x1, Pallas kernels, local(): pl.pallas_call(functools.partial(body, dims), out_shape=(jax.ShapeDtypeSt...  105 us
    unnamed x9, local copies, waits for them, and re-layouts  7.56 us

profile of v2, /device:TPU:1, one launch (start us, length us, event | category | flops | bytes accessed | tf_op | source)
XLA Modules:
  0.0 113.6 jit_solution(9614122505775646)
XLA Ops:
  0.6 105.4 %shard_map.119 = (bf16[8,8,16,96]{3,2,1,0:T(8,128)(2,1)}, bf16[8,8,16,96]{3,2,1,0:T(8,128)(2,1)}, f32[27,96,96]{2,1,0:T(8,128)}, f32[27,96,96]{2,1,0:T(8,128)}, f32[4,96]{1,0:T(4,128)}) custom-call(bf16[8,8,16,96]{3,2,1,0:T(8,128)(2,1)} %feat_in.1, s32[8,8]{1,0:T(8,128)} %ground_in.1, s32[8,8]{1,0:T(8,128)} %thick_in.1, bf16[27,96,96]{2,1,0:T(8,128)(2,1)} %w1_in.1, ...), custom_call_target="tpu_custom_call" | custom-call | tf_op jit(solution)/shard_map/pallas_call | solution.py:666
  106.0 1.7 %copy.18 = bf16[8,8,16,96]{3,2,1,0:T(8,128)(2,1)} copy(bf16[8,8,16,96]{3,2,1,0:T(8,128)(2,1)} %get-tuple-element.10) | data formatting | bytes 393216
  107.7 1.7 %copy.19 = bf16[8,8,16,96]{3,2,1,0:T(8,128)(2,1)} copy(bf16[8,8,16,96]{3,2,1,0:T(8,128)(2,1)} %get-tuple-element.11) | data formatting | bytes 393216
  109.4 0.0 copy-start
  109.4 2.6 %copy.20 = f32[27,96,96]{2,1,0:T(8,128)} copy(f32[27,96,96]{2,1,0:T(8,128)} %get-tuple-element.12) | data formatting | bytes 1990656
  112.0 0.0 copy-done
  112.0 0.0 copy-start.1
  112.0 1.1 copy.21
  113.0 0.0 copy-done.1
  113.0 0.6 copy.22
Async XLA Ops:
  109.4 2.6 %copy-start = (f32[27,96,96]{2,1,0:T(8,128)S(1)}, f32[27,96,96]{2,1,0:T(8,128)}, u32[]{:S(2)}) copy-start(f32[27,96,96]{2,1,0:T(8,128)} %get-tuple-element.13) | copy-start | bytes 2985988
  112.0 1.1 copy-start.1

commit v3 on v2

--- a/solution.py
+++ b/solution.py
@@ -12,6 +12,7 @@
 F32 = jnp.float32
 BF16 = jnp.bfloat16
 L = 128
+VMEM_BYTES = 63400000
 SIDES = [(dx, dy) for dx in (-1, 0, 1) for dy in (-1, 0, 1) if (dx, dy) != (0, 0)]
 
 
@@ -25,7 +26,7 @@
     result_out, gfeat_out, g1_out, g2_out, norm_out,
     feat_ref, cot_ref, w1_ref, w2_ref, gains_ref, shifts_ref, ground_ref, thick_ref,
     result_ref, gfeat_ref, g1_ref, g2_ref, norm_ref,
-    S, CT, Y1, Y2, D1, MK, N1, N2, D2,
+    HB, S, CT, Y1, Y2, D1, MK, N1, N2, D2,
     ZS, ZR, MZ, NZ1, NZ2, DZ2,
     V, PS, PH, PD2, PD1, DT, W1, W2, T1, T2, GS,
     STS, RA, RB,
@@ -106,10 +107,11 @@
             low = ground_ref[x, y]
             high = low + thick_ref[x, y]
             m = jnp.where((level >= low) & (level < high), 1.0, 0.0).astype(F32)
-            S[1 + x, 1 + y] = m
-            S[1 + x, 1 + y, :, 0:C] = m[:, 0:C] * feat_ref[x, y].astype(F32)
-            CT[1 + x, 1 + y] = jnp.zeros((Z, L), F32)
-            CT[1 + x, 1 + y, :, 0:C] = cot_ref[x, y].astype(F32)
+            m = m.astype(BF16)
+            HB[0, 1 + x, 1 + y] = m
+            HB[0, 1 + x, 1 + y, :, 0:C] = m[:, 0:C] * feat_ref[x, y]
+            HB[1, 1 + x, 1 + y] = jnp.zeros((Z, L), BF16)
+            HB[1, 1 + x, 1 + y, :, 0:C] = cot_ref[x, y]
         return carry
 
     lax.fori_loop(0, X, load_block, 0)
@@ -122,13 +124,13 @@
             return pl.ds(n if d > 0 else 1, 1)
         return pl.ds(0 if d > 0 else n + 1, 1)
 
-    def plane_copies(q, ref):
+    def plane_copies(q):
         out = []
         for k, (dx, dy) in enumerate(SIDES):
             out.append(
                 pltpu.make_async_remote_copy(
-                    src_ref=ref.at[cut(dx, X, True), cut(dy, Y, True)],
-                    dst_ref=ref.at[cut(dx, X, False), cut(dy, Y, False)],
+                    src_ref=HB.at[q, cut(dx, X, True), cut(dy, Y, True)],
+                    dst_ref=HB.at[q, cut(dx, X, False), cut(dy, Y, False)],
                     send_sem=hs.at[q, k],
                     recv_sem=hr.at[q, k],
                     device_id=side(dx, dy),
@@ -161,9 +163,17 @@
             c.wait()
 
     def send_faces(q, ref):
+        if q > 1:
+            for at in (0, XE - 1):
+                ref[at] = HB[q, at].astype(F32)
+            for at in (0, YE - 1):
+                ref[1 : 1 + X, at] = HB[q, 1 : 1 + X, at].astype(F32)
+
         def one(x, carry):
-            ZS[q, 0, x] = ref[x, :, 0, :]
-            ZS[q, 1, x] = ref[x, :, Z - 1, :]
+            if q <= 1:
+                ref[x] = HB[q, x].astype(F32)
+            ZS[q, 0, x] = ref[x, :, 0, :].astype(BF16)
+            ZS[q, 1, x] = ref[x, :, Z - 1, :].astype(BF16)
             return carry
 
         lax.fori_loop(0, XE, one, 0)
@@ -239,6 +249,10 @@
 
     def own(ref, h):
         return ref[pl.ds(1 + h * H, H), 1 : 1 + Y, :, :]
+
+    def keep(q, ref, h, v):
+        ref[pl.ds(1 + h * H, H), 1 : 1 + Y, :, :] = v
+        HB[q, pl.ds(1 + h * H, H), 1 : 1 + Y, :, :] = v.astype(BF16)
 
     def local_sum(terms):
         def one(x, carry):
@@ -361,7 +375,7 @@
 
         lax.fori_loop(0, 27, one, 0)
 
-    start_all(plane_copies(0, S))
+    start_all(plane_copies(0))
     for c in arrivals[4:7]:
         c.wait()
     GS[0:2, 0:C] = gains_ref[...]
@@ -385,10 +399,10 @@
         arrivals[7].wait()
         lax.fori_loop(0, 27, load_rest, 0)
 
-    wait_all(plane_copies(0, S))
+    wait_all(plane_copies(0))
     send_faces(0, S)
     wait_all(face_copies(0))
-    start_all(plane_copies(1, CT))
+    start_all(plane_copies(1))
 
     at_y = lax.broadcasted_iota(jnp.int32, (YE, L), 0)
     live_y = jnp.where(
@@ -409,11 +423,11 @@
         S[x] = s
         faces = []
         for k in range(2):
-            f = ZR[0, k, x]
+            f = ZR[0, k, x].astype(F32)
             mf = spread_lanes(f) * (live * live_z[k])
             MZ[k, x] = mf
             f = f * mf
-            ZR[0, k, x] = f
+            ZR[0, k, x] = f.astype(BF16)
             faces.append(f)
         put(PS, x, s, faces[0], faces[1])
         return carry
@@ -421,7 +435,7 @@
     lax.fori_loop(0, XE, first_input, 0)
 
     def keep_y1(h, y):
-        Y1[pl.ds(1 + h * H, H), 1 : 1 + Y, :, :] = y * own(MK, h)
+        keep(2, Y1, h, y * own(MK, h))
 
     convolve(PS, W1, False, keep_y1)
 
@@ -439,10 +453,10 @@
     def norm_exchange(k, q, ref, fill):
         rows = norm_begin(k, ref)
         sum_start(k, 0, rows)
-        start_all(plane_copies(q, ref))
+        start_all(plane_copies(q))
         rows = sum_wait(k, 0, True)
         sum_start(k, 1, rows)
-        wait_all(plane_copies(q, ref))
+        wait_all(plane_copies(q))
         send_faces(q, ref)
         fill()
         wait_all(face_copies(q))
@@ -451,7 +465,7 @@
         rstd = lax.rsqrt(rows[1] / rows[2] + 1e-05)
         return mean, rstd, rows[2]
 
-    wait_all(plane_copies(1, CT))
+    wait_all(plane_copies(1))
     send_faces(1, CT)
     mean1, rstd1, count = norm_exchange(0, 2, Y1, fill_weights)
     gain1, gain2, shift1, shift2 = GS[0:1], GS[1:2], GS[2:3], GS[3:4]
@@ -466,7 +480,7 @@
         N1[x] = n
         faces = []
         for k in range(2):
-            nf, hf = act(ZR[2, k, x], MZ[k, x])
+            nf, hf = act(ZR[2, k, x].astype(F32), MZ[k, x])
             NZ1[k, x] = nf
             faces.append(hf)
         put(PH, x, hidden, faces[0], faces[1])
@@ -475,7 +489,7 @@
     lax.fori_loop(0, XE, second_input, 0)
 
     def keep_y2(h, y):
-        Y2[pl.ds(1 + h * H, H), 1 : 1 + Y, :, :] = y * own(MK, h)
+        keep(3, Y2, h, y * own(MK, h))
 
     convolve(PH, W2, False, keep_y2)
     mean2, rstd2, _ = norm_exchange(1, 3, Y2, lambda: wait_all(face_copies(1)))
@@ -499,7 +513,8 @@
             result_ref[x - 1] = out[1 : 1 + Y, :, 0:C].astype(BF16)
 
         for k in range(2):
-            nf, _, df = outgoing(ZR[3, k, x], ZR[0, k, x] * inner, MZ[k, x], ZR[1, k, x])
+            y, s, ct = (ZR[q, k, x].astype(F32) for q in (3, 0, 1))
+            nf, _, df = outgoing(y, s * inner, MZ[k, x], ct)
             NZ2[k, x] = nf
             DZ2[k, x] = df
         return carry
@@ -531,19 +546,17 @@
     def keep_d1(h, v):
         pre = gain1 * own(N1, h) + shift1
         sig = sigmoid(pre)
-        D1[pl.ds(1 + h * H, H), 1 : 1 + Y, :, :] = (
-            v * own(MK, h) * (sig * (1.0 + pre * (1.0 - sig)))
-        )
+        keep(4, D1, h, v * own(MK, h) * (sig * (1.0 + pre * (1.0 - sig))))
 
     convolve(PD2, T2, True, keep_d1)
     rows = local_sum(lambda x: (mid(D1, x), mid(D1, x) * mid(N1, x)))
     sum_start(3, 0, rows)
-    start_all(plane_copies(4, D1))
+    start_all(plane_copies(4))
     prepare(PD2)
     products(1, PH, 0, 3)
     rows = sum_wait(3, 0, False)
     sum_start(3, 1, rows)
-    wait_all(plane_copies(4, D1))
+    wait_all(plane_copies(4))
     send_faces(4, D1)
     products(1, PH, 3, 9)
     grad_step(1, 0)
@@ -557,7 +570,7 @@
             return m * factor * (d - sum1 / count - n * cross1 / count)
 
         main = back(D1[x], N1[x], MK[x])
-        faces = [back(ZR[4, k, x], NZ1[k, x], MZ[k, x]) for k in range(2)]
+        faces = [back(ZR[4, k, x].astype(F32), NZ1[k, x], MZ[k, x]) for k in range(2)]
         put(PD1, x, main, faces[0], faces[1])
         return carry
 
@@ -596,6 +609,19 @@
     results.append(pltpu.make_async_copy(g1_ref, g1_out, outs.at[4]))
     results[4].start()
     for c in results:
+        c.wait()
+
+
+def hand_over(*refs):
+    ins, outs, held, (into, out) = refs[0:5], refs[5:10], refs[10:15], refs[15:17]
+    first = [pltpu.make_async_copy(a, b, into.at[i]) for i, (a, b) in enumerate(zip(ins, held))]
+    last = [pltpu.make_async_copy(a, b, out.at[i]) for i, (a, b) in enumerate(zip(held, outs))]
+    for c in first:
+        c.start()
+    for a, b in zip(first, last):
+        a.wait()
+        b.start()
+    for c in last:
         c.wait()
 
 
@@ -629,8 +655,9 @@
         pltpu.VMEM((27, C, C), F32),
         pltpu.VMEM((4, C), F32),
     ]
+    scratch += [pltpu.VMEM((5, XE, YE, Z, L), BF16)]
     scratch += [ext] * 9
-    scratch += [pltpu.VMEM((5, 2, XE, YE, L), F32)] * 2
+    scratch += [pltpu.VMEM((5, 2, XE, YE, L), BF16)] * 2
     scratch += [face] * 4
     scratch += [pltpu.VMEM((YE, Z + 16, L), F32)]
     scratch += [patch] * 4
@@ -663,22 +690,31 @@
     scratch += [dma((2, 7, 3 * most)), dma((2, 7, 3 * most))]
     scratch += [dma((8,)), dma((5,))]
     anywhere = pl.BlockSpec(memory_space=pl.ANY)
-    return pl.pallas_call(
+    shapes = (
+        jax.ShapeDtypeStruct((X, Y, Z, C), BF16),
+        jax.ShapeDtypeStruct((X, Y, Z, C), BF16),
+        jax.ShapeDtypeStruct((27, C, C), F32),
+        jax.ShapeDtypeStruct((27, C, C), F32),
+        jax.ShapeDtypeStruct((4, C), F32),
+    )
+    outs = pl.pallas_call(
         functools.partial(body, dims),
-        out_shape=(
-            jax.ShapeDtypeStruct((X, Y, Z, C), BF16),
-            jax.ShapeDtypeStruct((X, Y, Z, C), BF16),
-            jax.ShapeDtypeStruct((27, C, C), F32),
-            jax.ShapeDtypeStruct((27, C, C), F32),
-            jax.ShapeDtypeStruct((4, C), F32),
-        ),
-        in_specs=[anywhere] * 8,
+        out_shape=shapes,
+        in_specs=[pl.BlockSpec(memory_space=pltpu.HBM)] * 8,
         out_specs=(anywhere,) * 5,
         scratch_shapes=scratch,
         compiler_params=pltpu.CompilerParams(
-            collective_id=0, has_side_effects=True, vmem_limit_bytes=62 * 1024 * 1024
+            collective_id=0, has_side_effects=True, vmem_limit_bytes=VMEM_BYTES
         ),
     )(features, ground, thickness, weight_one, weight_two, gains, shifts, cotangent)
+    return pl.pallas_call(
+        hand_over,
+        out_shape=shapes,
+        in_specs=[anywhere] * 5,
+        out_specs=(pl.BlockSpec(memory_space=pltpu.HBM),) * 5,
+        scratch_shapes=[pltpu.VMEM(v.shape, v.dtype) for v in shapes] + [dma((5,)), dma((5,))],
+        compiler_params=pltpu.CompilerParams(vmem_limit_bytes=VMEM_BYTES),
+    )(*outs)
 
 
 def solution(mesh):

time: 114 us -> 106 us (0.930)
  local copies, waits for them, and re-layouts: 7.56 us -> 0 us
    unnamed x9 -> x0, local copies, waits for them, and re-layouts: 7.56 us -> none
    pallas_call x1 -> x2, Pallas kernels: 105 us -> 105 us  [the longest x1 102 us: local(): pl.pallas_call(functools.partial(body, dims), out_shape=shapes, in_specs=...]
where the time goes in v3:
time: 106 us
  Pallas kernels  105 us (99%)
    pallas_call x1, Pallas kernels, local(): pl.pallas_call(functools.partial(body, dims), out_shape=shapes, in_specs=...  102 us
    pallas_call x1, Pallas kernels, local(): pl.pallas_call(hand_over, out_shape=shapes, in_specs=[anywhere] * 5, out_...  3.08 us

profile of v3, /device:TPU:1, one launch (start us, length us, event | category | flops | bytes accessed | tf_op | source)
XLA Modules:
  0.0 105.6 jit_solution(3796170969752343618)
XLA Ops:
  0.6 101.9 %shard_map.119 = (bf16[8,8,16,96]{3,2,1,0:T(8,128)(2,1)}, bf16[8,8,16,96]{3,2,1,0:T(8,128)(2,1)}, f32[27,96,96]{2,1,0:T(8,128)}, f32[27,96,96]{2,1,0:T(8,128)}, f32[4,96]{1,0:T(4,128)}) custom-call(bf16[8,8,16,96]{3,2,1,0:T(8,128)(2,1)} %feat_in.1, s32[8,8]{1,0:T(8,128)} %ground_in.1, s32[8,8]{1,0:T(8,128)} %thick_in.1, bf16[27,96,96]{2,1,0:T(8,128)(2,1)} %w1_in.1, ...), custom_call_target="tpu_custom_call" | custom-call | tf_op jit(solution)/shard_map/pallas_call | solution.py:700
  102.5 3.1 %shard_map.120 = (bf16[8,8,16,96]{3,2,1,0:T(8,128)(2,1)}, bf16[8,8,16,96]{3,2,1,0:T(8,128)(2,1)}, f32[27,96,96]{2,1,0:T(8,128)}, f32[27,96,96]{2,1,0:T(8,128)}, f32[4,96]{1,0:T(4,128)}) custom-call(bf16[8,8,16,96]{3,2,1,0:T(8,128)(2,1)} %get-tuple-element.10.refs_0_, bf16[8,8,16,96]{3,2,1,0:T(8,128)(2,1)} %get-tuple-element.11.refs_1_, ...), custom_call_target="tpu_custom_call" | custom-call | tf_op jit(solution)/shard_map/pallas_call | solution.py:710

commit v4 on v3

--- a/solution.py
+++ b/solution.py
@@ -265,9 +265,9 @@
     def mid(ref, x):
         return ref[x, 1 : 1 + Y, :, :]
 
-    def prepare(dy):
-        flat = dy[1 : 1 + X, 1 : 1 + Y, :, L : 2 * L].reshape(X * Y * Z, L)
-        DT[...] = flat.T
+    def prepare(get):
+        for x in range(X):
+            DT[:, x * Y * Z : (x + 1) * Y * Z] = get(1 + x).reshape(Y * Z, L).astype(BF16).T
 
     def products(g, src, first, last):
         def one(k, carry):
@@ -275,7 +275,7 @@
             patch = src[pl.ds(a, X), pl.ds(b, Y), :, :].reshape(X * Y * Z, 3 * L)
             out = jnp.dot(DT[...], patch, preferred_element_type=F32)
             for c in range(3):
-                GA[g, pl.ds(pl.multiple_of((3 * k + c) * C, 8), C), :] = (
+                GA[g, pl.ds(pl.multiple_of((3 * k + c) * C, 16), C), :] = (
                     out[:, c * L : (c + 1) * L].T[0:C]
                 )
             return carry
@@ -293,15 +293,15 @@
     len_c = base
 
     def rows_at(off, n):
-        return pl.ds(pl.multiple_of(off, 8), n)
+        return pl.ds(pl.multiple_of(off, 16), n)
 
     most = max(n_y, n_z, NGY) - 1
 
     def grad_copies(g, stage):
         def copy(src, dst, k, other):
             return pltpu.make_async_remote_copy(
-                src_ref=src, dst_ref=dst, send_sem=gs.at[g, stage, k],
-                recv_sem=gr.at[g, stage, k], device_id=other, device_id_type=MESH,
+                src_ref=src, dst_ref=dst, send_sem=gs.at[g, k],
+                recv_sem=gr.at[g * 7 + stage if g < 2 else 6 + g * 4 + stage, k], device_id=other, device_id_type=MESH,
             )
 
         if stage == 0:
@@ -331,9 +331,11 @@
                 out.append(copy(part, land, p * most + j - 1, peer(j)))
         return out
 
-    def grad_step(g, stage):
+    def grad_step(g, stage, late=None):
         if stage > 0:
             wait_all(grad_copies(g, stage - 1))
+        if stage == 4:
+            wait_all(grad_copies(g + 2, 3))
         for p, (plan, base, len1, seg) in enumerate(plans):
             GB, GY, GD, GZ, GE, GX = portions[p]
             if stage == 1:
@@ -357,11 +359,14 @@
                 GE[g] = v
                 GX[g, plan[2][1]] = v
             if stage == 4:
-                v = GX[g, 0]
+                v, w = GX[g, 0], GX[g + 2, 0]
                 for j in range(1, plan[2][0]):
                     v = v + GX[g, j]
+                    w = w + GX[g + 2, j]
+                total, cross, factor = late
+                v = factor * (v - (total / count) * spread_lanes(w) - (cross / count) * w)
                 off = core * len_c + base + plan[0][1] * len1 + plan[1][1] * seg
-                GF[g, rows_at(off, seg)] = v
+                GF[g, rows_at(off, seg)] = v.astype(BF16)
         if stage < 7:
             start_all(grad_copies(g, stage))
 
@@ -370,7 +375,7 @@
 
     def grad_store(g, out_ref):
         def one(t, carry):
-            out_ref[t] = GF[g, rows_at(t * C, C)][:, 0:C] * scale
+            out_ref[t] = GF[g, rows_at(t * C, C)].astype(F32)[:, 0:C] * scale
             return carry
 
         lax.fori_loop(0, 27, one, 0)
@@ -492,7 +497,16 @@
         keep(3, Y2, h, y * own(MK, h))
 
     convolve(PH, W2, False, keep_y2)
-    mean2, rstd2, _ = norm_exchange(1, 3, Y2, lambda: wait_all(face_copies(1)))
+    spare = jnp.where(lax.broadcasted_iota(jnp.int32, (1, L), 1) == L - 1, 1.0, 0.0).astype(F32)
+
+    def second_fill():
+        wait_all(face_copies(1))
+        prepare(lambda x: mid(MK, x) * (mid(N1, x) + spare))
+        products(2, PS, 0, 9)
+        grad_step(2, 0)
+
+    mean2, rstd2, _ = norm_exchange(1, 3, Y2, second_fill)
+    grad_step(2, 1)
 
     def outgoing(y, s, m, ct):
         n = (y - mean2) * rstd2
@@ -525,10 +539,19 @@
     results[0].start()
 
     rows = local_sum(lambda x: (mid(D2, x), mid(D2, x) * mid(N2, x)))
-    for part in range(2):
-        sum_start(2, part, rows)
-        rows = sum_wait(2, part, False)
-    sum2, cross2 = rows
+    sum_start(2, 0, rows)
+    prepare(lambda x: mid(D2, x))
+    products(1, PH, 0, 7)
+    rows = sum_wait(2, 0, False)
+    sum_start(2, 1, rows)
+    products(1, PH, 7, 9)
+    grad_step(1, 0)
+    prepare(lambda x: mid(MK, x) * (mid(N2, x) + spare))
+    products(3, PH, 0, 9)
+    grad_step(2, 2)
+    sum2, cross2 = sum_wait(2, 1, False)
+    grad_step(1, 1)
+    grad_step(3, 0)
 
     def third_input(x, carry):
         factor = gain2 * rstd2
@@ -552,14 +575,19 @@
     rows = local_sum(lambda x: (mid(D1, x), mid(D1, x) * mid(N1, x)))
     sum_start(3, 0, rows)
     start_all(plane_copies(4))
-    prepare(PD2)
-    products(1, PH, 0, 3)
+    grad_step(3, 1)
+    prepare(lambda x: mid(D1, x))
+    products(0, PS, 0, 9)
+    grad_step(0, 0)
     rows = sum_wait(3, 0, False)
     sum_start(3, 1, rows)
     wait_all(plane_copies(4))
     send_faces(4, D1)
-    products(1, PH, 3, 9)
-    grad_step(1, 0)
+    grad_step(1, 2)
+    grad_step(2, 3)
+    grad_step(0, 1)
+    grad_step(3, 2)
+    grad_step(1, 3)
     wait_all(face_copies(4))
     sum1, cross1 = sum_wait(3, 1, False)
 
@@ -575,11 +603,6 @@
         return carry
 
     lax.fori_loop(0, XE, fourth_input, 0)
-    grad_step(1, 1)
-    prepare(PD1)
-    products(0, PS, 0, 9)
-    grad_step(0, 0)
-    grad_step(1, 2)
 
     def keep_features(h, v):
         out = own(MK, h) * (own(D2, h) + v)
@@ -597,14 +620,20 @@
     results[1].start()
     results[2].start()
 
-    for stage in range(1, 8):
-        grad_step(0, stage)
-        if stage + 2 < 8:
-            grad_step(1, stage + 2)
-        if stage == 6:
-            grad_store(1, g2_ref)
-            results.append(pltpu.make_async_copy(g2_ref, g2_out, outs.at[3]))
-            results[3].start()
+    grad_step(0, 2)
+    grad_step(3, 3)
+    grad_step(0, 3)
+    grad_step(1, 4, (sum2, cross2, gain2 * rstd2))
+    grad_step(0, 4, (sum1, cross1, gain1 * rstd1))
+    grad_step(1, 5)
+    grad_step(0, 5)
+    grad_step(1, 6)
+    grad_step(0, 6)
+    grad_step(1, 7)
+    grad_store(1, g2_ref)
+    results.append(pltpu.make_async_copy(g2_ref, g2_out, outs.at[3]))
+    results[3].start()
+    grad_step(0, 7)
     grad_store(0, g1_ref)
     results.append(pltpu.make_async_copy(g1_ref, g1_out, outs.at[4]))
     results[4].start()
@@ -631,8 +660,8 @@
     n_y, n_z = NGZ // 2, NGX
     n = (n_y, n_z, NGY)
     pairs = [n[p] * n[(p + 1) % 3] for p in range(3)]
-    tiles = -(-27 * C // (2 * 8 * min(pairs)))
-    segs = tuple(8 * (tiles // 3 + (p < tiles % 3)) for p in range(3))
+    tiles = -(-27 * C // (2 * 16 * min(pairs)))
+    segs = tuple(16 * (tiles // 3 + (p < tiles % 3)) for p in range(3))
     dims = (NGX, NGY, NGZ, X, Y, Z, C, segs)
     XE, YE = X + 2, Y + 2
     ext = pltpu.VMEM((XE, YE, Z, L), F32)
@@ -669,25 +698,25 @@
     scratch += [pltpu.VMEM((4, k, 4, L), F32) for k in (n_a, n_b)]
     len_c = sum(a * b for a, b in zip(pairs, segs))
     scratch += [
-        pltpu.VMEM((2, 2 * len_c, L), F32),
-        pltpu.VMEM((2, len_c, L), F32),
-        pltpu.VMEM((2, 2 * len_c, L), F32),
+        pltpu.VMEM((4, 2 * len_c, L), F32),
+        pltpu.VMEM((4, len_c, L), F32),
+        pltpu.VMEM((2, 2 * len_c, L), BF16),
     ]
     for p in range(3):
         n1, n2, n3 = n[p], n[(p + 1) % 3], n[(p + 2) % 3]
         seg = segs[p]
         scratch += [
-            pltpu.VMEM((2, n1 * n2 * seg, L), F32),
-            pltpu.VMEM((2, n1 - 1, n2 * seg, L), F32),
-            pltpu.VMEM((2, n2 * seg, L), F32),
-            pltpu.VMEM((2, n2 - 1, seg, L), F32),
-            pltpu.VMEM((2, seg, L), F32),
-            pltpu.VMEM((2, n3, seg, L), F32),
+            pltpu.VMEM((4, n1 * n2 * seg, L), F32),
+            pltpu.VMEM((4, n1 - 1, n2 * seg, L), F32),
+            pltpu.VMEM((4, n2 * seg, L), F32),
+            pltpu.VMEM((4, n2 - 1, seg, L), F32),
+            pltpu.VMEM((4, seg, L), F32),
+            pltpu.VMEM((4, n3, seg, L), F32),
         ]
     most = max(n) - 1
     scratch += [dma((5, 8)), dma((5, 8)), dma((5, 2)), dma((5, 2))]
     scratch += [dma((n_a + n_b,)), dma((4, n_a + n_b))]
-    scratch += [dma((2, 7, 3 * most)), dma((2, 7, 3 * most))]
+    scratch += [dma((4, 3 * most)), dma((22, 3 * most))]
     scratch += [dma((8,)), dma((5,))]
     anywhere = pl.BlockSpec(memory_space=pl.ANY)
     shapes = (

time: 106 us -> 99.4 us (0.938)
  Pallas kernels: 105 us -> 98.6 us
    pallas_call x1, Pallas kernels: 102 us -> 95.5 us  [local(): pl.pallas_call(functools.partial(body, dims), out_shape=shapes, in_specs=...]
where the time goes in v4:
time: 99.4 us; the launch traced here: 99.3 us
  Pallas kernels  98.6 us (99%)
    pallas_call x1, Pallas kernels, local(): pl.pallas_call(functools.partial(body, dims), out_shape=shapes, in_specs=...  95.5 us
    pallas_call x1, Pallas kernels, local(): pl.pallas_call(hand_over, out_shape=shapes, in_specs=[anywhere] * 5, out_...  3.08 us

profile of v4, /device:TPU:1, one launch (start us, length us, event | category | flops | bytes accessed | tf_op | source)
XLA Modules:
  0.0 99.3 jit_solution(644319510890876372)
XLA Ops:
  0.6 95.5 %shard_map.119 = (bf16[8,8,16,96]{3,2,1,0:T(8,128)(2,1)}, bf16[8,8,16,96]{3,2,1,0:T(8,128)(2,1)}, f32[27,96,96]{2,1,0:T(8,128)}, f32[27,96,96]{2,1,0:T(8,128)}, f32[4,96]{1,0:T(4,128)}) custom-call(bf16[8,8,16,96]{3,2,1,0:T(8,128)(2,1)} %feat_in.1, s32[8,8]{1,0:T(8,128)} %ground_in.1, s32[8,8]{1,0:T(8,128)} %thick_in.1, bf16[27,96,96]{2,1,0:T(8,128)(2,1)} %w1_in.1, ...), custom_call_target="tpu_custom_call" | custom-call | tf_op jit(solution)/shard_map/pallas_call | solution.py:729
  96.2 3.1 %shard_map.120 = (bf16[8,8,16,96]{3,2,1,0:T(8,128)(2,1)}, bf16[8,8,16,96]{3,2,1,0:T(8,128)(2,1)}, f32[27,96,96]{2,1,0:T(8,128)}, f32[27,96,96]{2,1,0:T(8,128)}, f32[4,96]{1,0:T(4,128)}) custom-call(bf16[8,8,16,96]{3,2,1,0:T(8,128)(2,1)} %get-tuple-element.10.refs_0_, bf16[8,8,16,96]{3,2,1,0:T(8,128)(2,1)} %get-tuple-element.11.refs_1_, ...), custom_call_target="tpu_custom_call" | custom-call | tf_op jit(solution)/shard_map/pallas_call | solution.py:739

commit v5 on v4

--- a/solution.py
+++ b/solution.py
@@ -14,6 +14,7 @@
 L = 128
 VMEM_BYTES = 63400000
 SIDES = [(dx, dy) for dx in (-1, 0, 1) for dy in (-1, 0, 1) if (dx, dy) != (0, 0)]
+FACES = [(k, dx, dy) for k in (0, 1) for dx in (-1, 0, 1) for dy in (-1, 0, 1)]
 
 
 def sigmoid(v):
@@ -27,7 +28,7 @@
     feat_ref, cot_ref, w1_ref, w2_ref, gains_ref, shifts_ref, ground_ref, thick_ref,
     result_ref, gfeat_ref, g1_ref, g2_ref, norm_ref,
     HB, S, CT, Y1, Y2, D1, MK, N1, N2, D2,
-    ZS, ZR, MZ, NZ1, NZ2, DZ2,
+    ZC, ZY, RC, RX, RY, RK, ZE, MZ, NZ1, NZ2, DZ2,
     V, PS, PH, PD2, PD1, DT, W1, W2, T1, T2, GS,
     STS, RA, RB,
     GA, GC, GF, *rest,
@@ -72,12 +73,14 @@
         other = (me_b + j) % n_b
         return dev(gx, other // n_y, (other % n_y) * 2 + z_hi)
 
-    down = dev(gx, gy, (gz + NGZ - 1) % NGZ)
-    up = dev(gx, gy, (gz + 1) % NGZ)
+    def beyond(k, dx, dy):
+        z = (gz + NGZ - 1) % NGZ if k == 0 else (gz + 1) % NGZ
+        return dev((gx + dx + NGX) % NGX, (gy + dy + NGY) % NGY, z)
+
 
     greet = [peer_a(j) for j in range(1, n_a)]
     greet += [peer_b(j) for j in range(1, n_b)]
-    greet += [down, up]
+    greet += [beyond(k, dx, dy) for k, dx, dy in FACES]
     greet += [side(dx, dy) for dx, dy in SIDES]
     barrier = pltpu.get_barrier_semaphore()
     for other in greet:
@@ -107,11 +110,12 @@
             low = ground_ref[x, y]
             high = low + thick_ref[x, y]
             m = jnp.where((level >= low) & (level < high), 1.0, 0.0).astype(F32)
-            m = m.astype(BF16)
-            HB[0, 1 + x, 1 + y] = m
-            HB[0, 1 + x, 1 + y, :, 0:C] = m[:, 0:C] * feat_ref[x, y]
-            HB[1, 1 + x, 1 + y] = jnp.zeros((Z, L), BF16)
-            HB[1, 1 + x, 1 + y, :, 0:C] = cot_ref[x, y]
+            S[1 + x, 1 + y] = m
+            S[1 + x, 1 + y, :, 0:C] = m[:, 0:C] * feat_ref[x, y].astype(F32)
+            CT[1 + x, 1 + y] = jnp.zeros((Z, L), F32)
+            CT[1 + x, 1 + y, :, 0:C] = cot_ref[x, y].astype(F32)
+            HB[0, 1 + x, 1 + y] = S[1 + x, 1 + y].astype(BF16)
+            HB[1, 1 + x, 1 + y] = CT[1 + x, 1 + y].astype(BF16)
         return carry
 
     lax.fori_loop(0, X, load_block, 0)
@@ -141,14 +145,24 @@
 
     def face_copies(q):
         out = []
-        for k, other in ((0, down), (1, up)):
+        for i, (k, dx, dy) in enumerate(FACES):
+            edge_x, side_x = (X - 1, 0) if dx > 0 else (0, 1)
+            edge_y, side_y = (1, 0) if dy > 0 else (0, 1)
+            if dx and dy:
+                src, dst = ZC.at[q, k, edge_x], RK.at[q, 1 - k, side_x, side_y]
+            elif dx:
+                src, dst = ZC.at[q, k, edge_x], RX.at[q, 1 - k, side_x]
+            elif dy:
+                src, dst = ZY.at[q, k, edge_y], RY.at[q, 1 - k, side_y]
+            else:
+                src, dst = ZC.at[q, k], RC.at[q, 1 - k]
             out.append(
                 pltpu.make_async_remote_copy(
-                    src_ref=ZS.at[q, k],
-                    dst_ref=ZR.at[q, 1 - k],
-                    send_sem=zs.at[q, k],
-                    recv_sem=zr.at[q, k],
-                    device_id=other,
+                    src_ref=src,
+                    dst_ref=dst,
+                    send_sem=zs.at[int(q == 1), i],
+                    recv_sem=zr.at[q, i],
+                    device_id=beyond(k, dx, dy),
                     device_id_type=MESH,
                 )
             )
@@ -162,22 +176,43 @@
         for c in copies:
             c.wait()
 
-    def send_faces(q, ref):
+    def halo_start(q, ref):
+        def one(x, carry):
+            for k, z in ((0, 0), (1, Z - 1)):
+                ZC[q, k, x] = ref[1 + x, 1 : 1 + Y, z, :].astype(BF16)
+            return carry
+
+        start_all(plane_copies(q))
+        lax.fori_loop(0, X, one, 0)
+        for k, z in ((0, 0), (1, Z - 1)):
+            for i, y in ((0, 1), (1, Y)):
+                ZY[q, k, i] = ref[1 : 1 + X, y, z, :].astype(BF16)
+        start_all(face_copies(q))
+
+    def halo_finish(q, ref):
+        wait_all(plane_copies(q))
+        wait_all(face_copies(q))
         if q > 1:
             for at in (0, XE - 1):
                 ref[at] = HB[q, at].astype(F32)
             for at in (0, YE - 1):
                 ref[1 : 1 + X, at] = HB[q, 1 : 1 + X, at].astype(F32)
-
-        def one(x, carry):
-            if q <= 1:
-                ref[x] = HB[q, x].astype(F32)
-            ZS[q, 0, x] = ref[x, :, 0, :].astype(BF16)
-            ZS[q, 1, x] = ref[x, :, Z - 1, :].astype(BF16)
-            return carry
-
-        lax.fori_loop(0, XE, one, 0)
-        start_all(face_copies(q))
+        for k in range(2):
+            def one(x, carry):
+                ZE[q, k, 1 + x, 1 : 1 + Y] = RC[q, k, x].astype(F32)
+                return carry
+
+            lax.fori_loop(0, X, one, 0)
+            for i, at_x in ((0, 0), (1, XE - 1)):
+                ZE[q, k, at_x, 1 : 1 + Y] = RX[q, k, i].astype(F32)
+                for j, at_y in ((0, 0), (1, YE - 1)):
+                    row = Y - 1 if j == 0 else 0
+                    tile = RK[q, k, i, j].astype(F32)
+                    ZE[q, k, at_x, at_y : at_y + 1] = tile[row : row + 1]
+            for j, at_y in ((0, 0), (1, YE - 1)):
+                tile = RY[q, k, j].astype(F32)
+                for x in range(X):
+                    ZE[q, k, 1 + x, at_y : at_y + 1] = tile[x : x + 1]
 
     def sum_copies(k, part):
         n, me, peer, land = ((n_a, me_a, peer_a, RA), (n_b, me_b, peer_b, RB))[part]
@@ -380,7 +415,7 @@
 
         lax.fori_loop(0, 27, one, 0)
 
-    start_all(plane_copies(0))
+    halo_start(0, S)
     for c in arrivals[4:7]:
         c.wait()
     GS[0:2, 0:C] = gains_ref[...]
@@ -404,10 +439,8 @@
         arrivals[7].wait()
         lax.fori_loop(0, 27, load_rest, 0)
 
-    wait_all(plane_copies(0))
-    send_faces(0, S)
-    wait_all(face_copies(0))
-    start_all(plane_copies(1))
+    halo_finish(0, S)
+    halo_start(1, CT)
 
     at_y = lax.broadcasted_iota(jnp.int32, (YE, L), 0)
     live_y = jnp.where(
@@ -421,18 +454,18 @@
     def first_input(x, carry):
         gone = ((x == 0) & (gx == 0)) | ((x == XE - 1) & (gx == NGX - 1))
         live = live_y * jnp.where(gone, 0.0, 1.0)
-        s = S[x]
+        s = HB[0, x].astype(F32)
         m = spread_lanes(s) * live[:, None, :]
         MK[x] = m
         s = s * m
         S[x] = s
         faces = []
         for k in range(2):
-            f = ZR[0, k, x].astype(F32)
+            f = ZE[0, k, x]
             mf = spread_lanes(f) * (live * live_z[k])
             MZ[k, x] = mf
             f = f * mf
-            ZR[0, k, x] = f.astype(BF16)
+            ZE[0, k, x] = f
             faces.append(f)
         put(PS, x, s, faces[0], faces[1])
         return carry
@@ -458,20 +491,16 @@
     def norm_exchange(k, q, ref, fill):
         rows = norm_begin(k, ref)
         sum_start(k, 0, rows)
-        start_all(plane_copies(q))
+        halo_start(q, ref)
         rows = sum_wait(k, 0, True)
         sum_start(k, 1, rows)
-        wait_all(plane_copies(q))
-        send_faces(q, ref)
         fill()
-        wait_all(face_copies(q))
+        halo_finish(q, ref)
         rows = sum_wait(k, 1, True)
         mean = rows[0] / rows[2]
         rstd = lax.rsqrt(rows[1] / rows[2] + 1e-05)
         return mean, rstd, rows[2]
 
-    wait_all(plane_copies(1))
-    send_faces(1, CT)
     mean1, rstd1, count = norm_exchange(0, 2, Y1, fill_weights)
     gain1, gain2, shift1, shift2 = GS[0:1], GS[1:2], GS[2:3], GS[3:4]
 
@@ -485,7 +514,7 @@
         N1[x] = n
         faces = []
         for k in range(2):
-            nf, hf = act(ZR[2, k, x].astype(F32), MZ[k, x])
+            nf, hf = act(ZE[2, k, x], MZ[k, x])
             NZ1[k, x] = nf
             faces.append(hf)
         put(PH, x, hidden, faces[0], faces[1])
@@ -500,13 +529,12 @@
     spare = jnp.where(lax.broadcasted_iota(jnp.int32, (1, L), 1) == L - 1, 1.0, 0.0).astype(F32)
 
     def second_fill():
-        wait_all(face_copies(1))
+        halo_finish(1, CT)
         prepare(lambda x: mid(MK, x) * (mid(N1, x) + spare))
         products(2, PS, 0, 9)
         grad_step(2, 0)
 
     mean2, rstd2, _ = norm_exchange(1, 3, Y2, second_fill)
-    grad_step(2, 1)
 
     def outgoing(y, s, m, ct):
         n = (y - mean2) * rstd2
@@ -518,7 +546,7 @@
     inner = jnp.where(lane < C, 1.0, 0.0).astype(F32)
 
     def last_forward(x, carry):
-        n, out, d = outgoing(Y2[x], S[x] * inner, MK[x], CT[x])
+        n, out, d = outgoing(Y2[x], S[x] * inner, MK[x], HB[1, x].astype(F32))
         N2[x] = n
         D2[x] = d
 
@@ -527,7 +555,7 @@
             result_ref[x - 1] = out[1 : 1 + Y, :, 0:C].astype(BF16)
 
         for k in range(2):
-            y, s, ct = (ZR[q, k, x].astype(F32) for q in (3, 0, 1))
+            y, s, ct = (ZE[q, k, x] for q in (3, 0, 1))
             nf, _, df = outgoing(y, s * inner, MZ[k, x], ct)
             NZ2[k, x] = nf
             DZ2[k, x] = df
@@ -540,6 +568,7 @@
 
     rows = local_sum(lambda x: (mid(D2, x), mid(D2, x) * mid(N2, x)))
     sum_start(2, 0, rows)
+    grad_step(2, 1)
     prepare(lambda x: mid(D2, x))
     products(1, PH, 0, 7)
     rows = sum_wait(2, 0, False)
@@ -574,21 +603,19 @@
     convolve(PD2, T2, True, keep_d1)
     rows = local_sum(lambda x: (mid(D1, x), mid(D1, x) * mid(N1, x)))
     sum_start(3, 0, rows)
-    start_all(plane_copies(4))
+    halo_start(4, D1)
     grad_step(3, 1)
     prepare(lambda x: mid(D1, x))
     products(0, PS, 0, 9)
     grad_step(0, 0)
     rows = sum_wait(3, 0, False)
     sum_start(3, 1, rows)
-    wait_all(plane_copies(4))
-    send_faces(4, D1)
     grad_step(1, 2)
     grad_step(2, 3)
     grad_step(0, 1)
     grad_step(3, 2)
     grad_step(1, 3)
-    wait_all(face_copies(4))
+    halo_finish(4, D1)
     sum1, cross1 = sum_wait(3, 1, False)
 
     def fourth_input(x, carry):
@@ -598,7 +625,7 @@
             return m * factor * (d - sum1 / count - n * cross1 / count)
 
         main = back(D1[x], N1[x], MK[x])
-        faces = [back(ZR[4, k, x].astype(F32), NZ1[k, x], MZ[k, x]) for k in range(2)]
+        faces = [back(ZE[4, k, x], NZ1[k, x], MZ[k, x]) for k in range(2)]
         put(PD1, x, main, faces[0], faces[1])
         return carry
 
@@ -686,7 +713,15 @@
     ]
     scratch += [pltpu.VMEM((5, XE, YE, Z, L), BF16)]
     scratch += [ext] * 9
-    scratch += [pltpu.VMEM((5, 2, XE, YE, L), BF16)] * 2
+    scratch += [
+        pltpu.VMEM((5, 2, X, Y, L), BF16),
+        pltpu.VMEM((5, 2, 2, X, L), BF16),
+        pltpu.VMEM((5, 2, X, Y, L), BF16),
+        pltpu.VMEM((5, 2, 2, Y, L), BF16),
+        pltpu.VMEM((5, 2, 2, X, L), BF16),
+        pltpu.VMEM((5, 2, 2, 2, Y, L), BF16),
+        pltpu.VMEM((5, 2, XE, YE, L), F32),
+    ]
     scratch += [face] * 4
     scratch += [pltpu.VMEM((YE, Z + 16, L), F32)]
     scratch += [patch] * 4
@@ -714,7 +749,7 @@
             pltpu.VMEM((4, n3, seg, L), F32),
         ]
     most = max(n) - 1
-    scratch += [dma((5, 8)), dma((5, 8)), dma((5, 2)), dma((5, 2))]
+    scratch += [dma((5, 8)), dma((5, 8)), dma((2, 18)), dma((5, 18))]
     scratch += [dma((n_a + n_b,)), dma((4, n_a + n_b))]
     scratch += [dma((4, 3 * most)), dma((22, 3 * most))]
     scratch += [dma((8,)), dma((5,))]

time: 99.4 us -> 92.1 us (0.927)
  Pallas kernels: 98.6 us -> 91.3 us
    pallas_call x1, Pallas kernels: 95.5 us -> 88.2 us  [local(): pl.pallas_call(functools.partial(body, dims), out_shape=shapes, in_specs=...]
where the time goes in v5:
time: 92.1 us; the launch traced here: 92 us
  Pallas kernels  91.3 us (99%)
    pallas_call x1, Pallas kernels, local(): pl.pallas_call(functools.partial(body, dims), out_shape=shapes, in_specs=...  88.2 us
    pallas_call x1, Pallas kernels, local(): pl.pallas_call(hand_over, out_shape=shapes, in_specs=[anywhere] * 5, out_...  3.08 us

profile of v5, /device:TPU:1, one launch (start us, length us, event | category | flops | bytes accessed | tf_op | source)
XLA Modules:
  0.0 92.0 jit_solution(7029618966408351442)
XLA Ops:
  0.6 88.2 %shard_map.119 = (bf16[8,8,16,96]{3,2,1,0:T(8,128)(2,1)}, bf16[8,8,16,96]{3,2,1,0:T(8,128)(2,1)}, f32[27,96,96]{2,1,0:T(8,128)}, f32[27,96,96]{2,1,0:T(8,128)}, f32[4,96]{1,0:T(4,128)}) custom-call(bf16[8,8,16,96]{3,2,1,0:T(8,128)(2,1)} %feat_in.1, s32[8,8]{1,0:T(8,128)} %ground_in.1, s32[8,8]{1,0:T(8,128)} %thick_in.1, bf16[27,96,96]{2,1,0:T(8,128)(2,1)} %w1_in.1, ...), custom_call_target="tpu_custom_call" | custom-call | tf_op jit(solution)/shard_map/pallas_call | solution.py:764
  88.9 3.1 %shard_map.120 = (bf16[8,8,16,96]{3,2,1,0:T(8,128)(2,1)}, bf16[8,8,16,96]{3,2,1,0:T(8,128)(2,1)}, f32[27,96,96]{2,1,0:T(8,128)}, f32[27,96,96]{2,1,0:T(8,128)}, f32[4,96]{1,0:T(4,128)}) custom-call(bf16[8,8,16,96]{3,2,1,0:T(8,128)(2,1)} %get-tuple-element.10.refs_0_, bf16[8,8,16,96]{3,2,1,0:T(8,128)(2,1)} %get-tuple-element.11.refs_1_, ...), custom_call_target="tpu_custom_call" | custom-call | tf_op jit(solution)/shard_map/pallas_call | solution.py:774

commit v6 on v5

--- a/solution.py
+++ b/solution.py
@@ -315,7 +315,7 @@
                 )
             return carry
 
-        lax.fori_loop(first, last, one, 0)
+        lax.fori_loop(first, last, one, 0, unroll=True)
 
     axes = ((n_y, row_y, grad_y), (n_z, pos_z, grad_z), (NGY, gy, peer_y))
     plans = []
@@ -470,7 +470,7 @@
         put(PS, x, s, faces[0], faces[1])
         return carry
 
-    lax.fori_loop(0, XE, first_input, 0)
+    lax.fori_loop(0, XE, first_input, 0, unroll=2)
 
     def keep_y1(h, y):
         keep(2, Y1, h, y * own(MK, h))
@@ -520,7 +520,7 @@
         put(PH, x, hidden, faces[0], faces[1])
         return carry
 
-    lax.fori_loop(0, XE, second_input, 0)
+    lax.fori_loop(0, XE, second_input, 0, unroll=2)
 
     def keep_y2(h, y):
         keep(3, Y2, h, y * own(MK, h))
@@ -561,7 +561,7 @@
             DZ2[k, x] = df
         return carry
 
-    lax.fori_loop(0, XE, last_forward, 0)
+    lax.fori_loop(0, XE, last_forward, 0, unroll=2)
 
     results = [pltpu.make_async_copy(result_ref, result_out, outs.at[0])]
     results[0].start()
@@ -593,7 +593,7 @@
         put(PD2, x, main, faces[0], faces[1])
         return carry
 
-    lax.fori_loop(0, XE, third_input, 0)
+    lax.fori_loop(0, XE, third_input, 0, unroll=2)
 
     def keep_d1(h, v):
         pre = gain1 * own(N1, h) + shift1
@@ -629,7 +629,7 @@
         put(PD1, x, main, faces[0], faces[1])
         return carry
 
-    lax.fori_loop(0, XE, fourth_input, 0)
+    lax.fori_loop(0, XE, fourth_input, 0, unroll=2)
 
     def keep_features(h, v):
         out = own(MK, h) * (own(D2, h) + v)

time: 92.1 us -> 90.9 us (0.987)
  Pallas kernels: 91.3 us -> 90 us
    pallas_call x1, Pallas kernels: 88.2 us -> 86.9 us  [local(): pl.pallas_call(functools.partial(body, dims), out_shape=shapes, in_specs=...]
where the time goes in v6:
time: 90.9 us; the launch traced here: 90.8 us
  Pallas kernels  90 us (99%)
    pallas_call x1, Pallas kernels, local(): pl.pallas_call(functools.partial(body, dims), out_shape=shapes, in_specs=...  86.9 us
    pallas_call x1, Pallas kernels, local(): pl.pallas_call(hand_over, out_shape=shapes, in_specs=[anywhere] * 5, out_...  3.08 us

profile of v6, /device:TPU:1, one launch (start us, length us, event | category | flops | bytes accessed | tf_op | source)
XLA Modules:
  0.0 90.8 jit_solution(1373404775495987754)
XLA Ops:
  0.6 86.9 %shard_map.119 = (bf16[8,8,16,96]{3,2,1,0:T(8,128)(2,1)}, bf16[8,8,16,96]{3,2,1,0:T(8,128)(2,1)}, f32[27,96,96]{2,1,0:T(8,128)}, f32[27,96,96]{2,1,0:T(8,128)}, f32[4,96]{1,0:T(4,128)}) custom-call(bf16[8,8,16,96]{3,2,1,0:T(8,128)(2,1)} %feat_in.1, s32[8,8]{1,0:T(8,128)} %ground_in.1, s32[8,8]{1,0:T(8,128)} %thick_in.1, bf16[27,96,96]{2,1,0:T(8,128)(2,1)} %w1_in.1, ...), custom_call_target="tpu_custom_call" | custom-call | tf_op jit(solution)/shard_map/pallas_call | solution.py:764
  87.5 3.1 %shard_map.120 = (bf16[8,8,16,96]{3,2,1,0:T(8,128)(2,1)}, bf16[8,8,16,96]{3,2,1,0:T(8,128)(2,1)}, f32[27,96,96]{2,1,0:T(8,128)}, f32[27,96,96]{2,1,0:T(8,128)}, f32[4,96]{1,0:T(4,128)}) custom-call(bf16[8,8,16,96]{3,2,1,0:T(8,128)(2,1)} %get-tuple-element.10.refs_0_, bf16[8,8,16,96]{3,2,1,0:T(8,128)(2,1)} %get-tuple-element.11.refs_1_, ...), custom_call_target="tpu_custom_call" | custom-call | tf_op jit(solution)/shard_map/pallas_call | solution.py:774
